TPU v7x, 128 devices: a whole 4x4x4 slice. The times are simulated.
128 devices in a mesh: group: 4 (over z), local: 32 (over x, y, core).
Axes of the slice: x: 4, y: 4, z: 4, core: 2. Of those that a mesh axis runs over, the one named last changes fastest.
Arguments:
- token_codes: bfloat16 [16384, 3584], P(('group', 'local')), may hold values from -6 to 6
- block_scales: float32 [16384, 28], P(('group', 'local')), may hold values from 0.3 to 3
- route_scores: float32 [16384, 4], P(('group', 'local')), may hold values from -5 to 5
- expert_ids: int32 [16384, 4], P(('group', 'local')), may hold values from 0 to 127, as said below
- w_gate: bfloat16 [128, 3584, 1024], P(('group', 'local')), may hold values from -0.09375 to 0.09375
- w_up: bfloat16 [128, 3584, 1024], P(('group', 'local')), may hold values from -0.09375 to 0.09375
- w_down: bfloat16 [128, 1024, 3584], P(('group', 'local')), may hold values from -0.1875 to 0.1875
- teacher: bfloat16 [16384, 3584], P(('group', 'local')), may hold values from -6 to 6
Outputs:
- student_out: bfloat16 [16384, 3584], P(('group', 'local'))
- grad_tokens: bfloat16 [16384, 3584], P(('group', 'local'))
- grad_scores: float32 [16384, 4], P(('group', 'local'))
Inputs may be any that keep to these rules, and one draw needn't show every extreme that they name: `expert_ids`: each row names 4 different experts, all lying in at most 2 of the 4 groups, expert e belonging to group e // 32.
All inputs are finite; a program needn't handle non-finite values.
Results may differ from a plain program's by a relative error of at most 0.022.
Values may be sent and summed in bfloat16 or wider, within the bound.
No kernel may reach another device: no remote copies, remote signals or barrier semaphores. Data moves between devices by JAX's collectives and lax.ppermute only.
A program may use at most 192 MiB of HBM per device.

v0:
```python
import jax
import jax.numpy as jnp
from jax import lax
from jax.sharding import PartitionSpec as P

CONTRACT_LAST = (((1,), (1,)), ((), ()))


def silu_slope(values):
    gate_sigma = jax.nn.sigmoid(values)
    return gate_sigma * (1.0 + values * (1.0 - gate_sigma))


def expert_pre(in_rows, gate_mat, up_mat):
    leading = in_rows.shape[:-1]
    flat_rows = in_rows.reshape(-1, in_rows.shape[-1])
    pre_gate = jnp.dot(flat_rows, gate_mat, preferred_element_type=jnp.float32)
    pre_up = jnp.dot(flat_rows, up_mat, preferred_element_type=jnp.float32)
    return (pre_gate.reshape(leading + (-1,)), pre_up.reshape(leading + (-1,)))


def expert_out(pre_gate, pre_up, down_mat):
    leading = pre_gate.shape[:-1]
    active = (jax.nn.silu(pre_gate) * pre_up).astype(jnp.bfloat16).reshape(-1, pre_gate.shape[-1])
    outputs = jnp.dot(active, down_mat, preferred_element_type=jnp.float32).astype(jnp.bfloat16)
    return outputs.reshape(leading + (-1,))


def expert_back(grad_rows, pre_gate, pre_up, gate_mat, up_mat, down_mat):
    leading = grad_rows.shape[:-1]
    hidden_count = pre_gate.shape[-1]
    flat_grad = grad_rows.reshape(-1, grad_rows.shape[-1])
    gate_flat = pre_gate.reshape(-1, hidden_count)
    up_flat = pre_up.reshape(-1, hidden_count)
    grad_act = lax.dot_general(
        flat_grad, down_mat, CONTRACT_LAST, preferred_element_type=jnp.float32
    )
    grad_up = (grad_act * jax.nn.silu(gate_flat)).astype(jnp.bfloat16)
    grad_gate = (grad_act * up_flat * silu_slope(gate_flat)).astype(jnp.bfloat16)
    summed = lax.dot_general(grad_gate, gate_mat, CONTRACT_LAST, preferred_element_type=jnp.float32)
    summed = summed + lax.dot_general(
        grad_up, up_mat, CONTRACT_LAST, preferred_element_type=jnp.float32
    )
    return summed.astype(jnp.bfloat16).reshape(leading + (-1,))


def token_slots(expert_ids, capacity, experts):
    expert_range = jnp.arange(experts, dtype=jnp.int32)
    expert_hits = jnp.sum((expert_ids[:, :, None] == expert_range).astype(jnp.int32), axis=1)
    before = jnp.cumsum(expert_hits, axis=0) - expert_hits
    position = jnp.take_along_axis(before, expert_ids, axis=1)
    return (position, position < capacity)


def unpack_table(slot_table, top_count):
    is_valid = slot_table >= 0
    safe_code = jnp.where(is_valid, slot_table, 0)
    return (is_valid, safe_code, safe_code // top_count)


def group_sum(group_parts, axis_num):
    return jnp.sum(group_parts.astype(jnp.float32), axis=axis_num).astype(jnp.bfloat16)


def per_device(token_codes, block_scales, route_scores, expert_ids, w_gate, w_up, w_down, teacher):
    tok_count, feat_width = token_codes.shape
    top_count = expert_ids.shape[1]
    group_count = lax.axis_size("group")
    local_count = lax.axis_size("local")
    devices = group_count * local_count
    capacity = max(2, 5 * tok_count * top_count // (4 * devices))
    blocks = block_scales.shape[1]
    tokens_x = (
        (token_codes.astype(jnp.float32).reshape(tok_count, blocks, -1) * block_scales[:, :, None])
        .reshape(tok_count, feat_width)
        .astype(jnp.bfloat16)
    )
    gate_sigma = jax.nn.sigmoid(route_scores)
    sigma_sum = jnp.sum(gate_sigma, axis=1, keepdims=True)
    weights = (2.5 * gate_sigma / sigma_sum).astype(jnp.bfloat16)
    weight_f = weights.astype(jnp.float32)
    position, is_kept = token_slots(expert_ids, capacity, devices)
    kept_f = is_kept.astype(jnp.float32)
    gate_mat = w_gate[0]
    up_mat = w_up[0]
    down_mat = w_down[0]
    group_range = jnp.arange(group_count, dtype=jnp.int32)
    member = ((expert_ids // local_count)[:, :, None] == group_range) & is_kept[:, :, None]
    member_f = member.astype(jnp.float32)
    zero_bf = jnp.zeros((), jnp.bfloat16)
    slot_index = jnp.where(is_kept, expert_ids * capacity + position, devices * capacity)
    slot_codes = jnp.arange(tok_count * top_count, dtype=jnp.int32)
    slot_table = (
        jnp.full((devices * capacity,), -1, jnp.int32)
        .at[slot_index.reshape(-1)]
        .set(slot_codes, mode="drop")
    )
    is_valid, safe_code, token_pos = unpack_table(slot_table, top_count)
    send_rows = jnp.where(is_valid[:, None], tokens_x[token_pos], zero_bf).reshape(
        devices, capacity, feat_width
    )
    in_rows = lax.all_to_all(send_rows, ("group", "local"), split_axis=0, concat_axis=0, tiled=True)
    pre_gate, pre_up = expert_pre(in_rows, gate_mat, up_mat)
    outputs = expert_out(pre_gate, pre_up, down_mat)
    stashed = (outputs, in_rows, pre_gate, pre_up)
    returned = lax.all_to_all(
        stashed[0], ("group", "local"), split_axis=0, concat_axis=0, tiled=True
    ).reshape(devices * capacity, feat_width)
    lookup = jnp.where(is_kept, expert_ids * capacity + position, 0)
    outputs = returned[lookup].astype(jnp.float32)
    mix_weights = member_f * (weight_f * kept_f)[:, :, None]
    group_parts = jnp.einsum("tkg,tkd->gtd", mix_weights, outputs, precision=lax.Precision.HIGHEST)
    student_out = group_sum(lax.optimization_barrier(group_parts.astype(jnp.bfloat16)), 0)
    grad_y = (student_out.astype(jnp.float32) - teacher.astype(jnp.float32)).astype(jnp.bfloat16)
    upstream = grad_y.astype(jnp.float32)
    grad_w = jnp.sum(upstream[:, None, :] * outputs, axis=2) * kept_f
    slot_scale = jnp.where(is_valid, weight_f.reshape(-1)[safe_code], 0.0)
    grad_send = (
        (slot_scale[:, None] * upstream[token_pos])
        .astype(jnp.bfloat16)
        .reshape(devices, capacity, feat_width)
    )
    grad_in = lax.all_to_all(grad_send, ("group", "local"), split_axis=0, concat_axis=0, tiled=True)
    pre_gate = stashed[2]
    pre_up = stashed[3]
    grad_rows = expert_back(grad_in, pre_gate, pre_up, gate_mat, up_mat, down_mat)
    grad_ret = lax.all_to_all(
        grad_rows, ("group", "local"), split_axis=0, concat_axis=0, tiled=True
    ).reshape(devices * capacity, feat_width)
    grad_parts = jnp.einsum(
        "tkg,tkd->gtd",
        member_f,
        grad_ret[lookup].astype(jnp.float32),
        precision=lax.Precision.HIGHEST,
    )
    grad_tokens = group_sum(lax.optimization_barrier(grad_parts.astype(jnp.bfloat16)), 0)
    inner_sum = jnp.sum(grad_w * gate_sigma, axis=1, keepdims=True)
    grad_scores = (
        2.5
        * gate_sigma
        * (1.0 - gate_sigma)
        * (grad_w / sigma_sum - inner_sum / (sigma_sum * sigma_sum))
    )
    return (student_out, grad_tokens, grad_scores)


def solution(mesh):
    in_specs = (
        P(("group", "local"), None),
        P(("group", "local"), None),
        P(("group", "local"), None),
        P(("group", "local"), None),
        P(("group", "local"), None, None),
        P(("group", "local"), None, None),
        P(("group", "local"), None, None),
        P(("group", "local"), None),
    )
    out_specs = (
        P(("group", "local"), None),
        P(("group", "local"), None),
        P(("group", "local"), None),
    )
    return jax.shard_map(
        per_device, mesh=mesh, in_specs=in_specs, out_specs=out_specs, check_vma=False
    )
```

profile of v0, /device:TPU:1, one launch (start us, length us, event | category | flops | bytes accessed | tf_op | source)
XLA Modules:
  0.0 612.5 jit_solution(2325576277301579962)
XLA Ops:
  14.5 5.2 gather_fusion
  19.7 7.8 %gather.25 = bf16[128,5,3584]{2,1,0:T(8,128)(2,1)} reshape(bf16[640,3584]{1,0:T(8,128)(2,1)} %gather_fusion) | data formatting | bytes 9175040 | tf_op jit(solution)/shard_map/gather | solution.py:99
  31.3 98.3 %all_to_all.20 = bf16[128,5,3584]{2,1,0:T(8,128)(2,1)} all-to-all(bf16[128,5,3584]{2,1,0:T(8,128)(2,1)S(1)} %broadcast_select_fusion), channel_id=1, replica_groups=mesh['group'=4,'local'=32] {'group','local'}, dimensions={0} | all-to-all | bytes 9175040 | tf_op jit(solution)/shard_map/all_to_all | solution.py:102
  129.6 8.1 %reshape.109 = bf16[640,3584]{1,0:T(8,128)(2,1)} reshape(bf16[128,5,3584]{2,1,0:T(8,128)(2,1)} %all_to_all.20) | data formatting | bytes 9175040 | tf_op jit(solution)/shard_map/reshape | solution.py:16
  137.7 8.6 %fusion.10 = f32[640,1024]{1,0:T(8,128)S(1)} fusion(bf16[640,3584]{1,0:T(8,128)(2,1)} %reshape.109, bf16[1,3584,1024]{2,1,0:T(8,128)(2,1)} %param.12), kind=kOutput, calls=%fused_computation.19 | convolution fusion | flops 4697620480 | bytes 14548992 | tf_op jit(solution)/shard_map/dot_general | solution.py:17
  146.4 8.1 %fusion.6 = f32[640,1024]{1,0:T(8,128)S(1)} fusion(bf16[640,3584]{1,0:T(8,128)(2,1)S(1)} %copy-done, bf16[1,3584,1024]{2,1,0:T(8,128)(2,1)} %param.13), kind=kOutput, calls=%fused_computation.15 | convolution fusion | flops 4697620480 | bytes 14548992 | tf_op jit(solution)/shard_map/dot_general | solution.py:18
  156.0 7.4 %fusion.12 = bf16[640,3584]{1,0:T(8,128)(2,1)} fusion(bf16[1,1024,3584]{2,1,0:T(8,128)(2,1)S(1)} %bitcast.37, f32[640,1024]{1,0:T(8,128)S(1)} %fusion.6, f32[640,1024]{1,0:T(8,128)S(1)} %fusion.10), kind=kOutput, calls=%fused_computation.23 | convolution fusion | flops 4703846400 | bytes 17170432 | tf_op jit(solution)/shard_map/dot_general | solution.py:25
  163.4 7.8 %reshape.110 = bf16[128,5,3584]{2,1,0:T(8,128)(2,1)} reshape(bf16[640,3584]{1,0:T(8,128)(2,1)} %fusion.12) | data formatting | bytes 9175040 | tf_op jit(solution)/shard_map/reshape | solution.py:26
  171.2 5.7 all-to-all-start.1
  177.8 4.3 gather_fusion.2
  182.4 81.2 %all-to-all-done.1 = bf16[128,5,3584]{2,1,0:T(8,128)(2,1)} async-done(((bf16[128,5,3584]{2,1,0:T(8,128)(2,1)}), bf16[128,5,3584]{2,1,0:T(8,128)(2,1)}, u32[]{:S(2)}, u32[]{:S(2)}) %all-to-all-start.1) | async-done | bytes 4587552 | tf_op jit(solution)/shard_map/all_to_all | solution.py:106
  263.6 8.1 %reshape.111 = bf16[640,3584]{1,0:T(8,128)(2,1)} reshape(bf16[128,5,3584]{2,1,0:T(8,128)(2,1)} %all-to-all-done.1) | data formatting | bytes 9175040 | tf_op jit(solution)/shard_map/reshape | solution.py:108
  271.7 10.8 %gather_fusion.1 = bf16[512,3584]{1,0:T(8,128)(2,1)} fusion(bf16[640,3584]{1,0:T(8,128)(2,1)} %reshape.111, s32[1024]{0:T(1024)S(1)} %pad_clamp_fusion.1), kind=kCustom, calls=%fused_computation.1 | custom fusion | bytes 7342080 | tf_op jit(solution)/shard_map/gather | solution.py:110
  282.5 7.0 %reshape.125 = bf16[128,4,3584]{2,1,0:T(4,128)(2,1)} reshape(bf16[512,3584]{1,0:T(8,128)(2,1)} %gather_fusion.1) | data formatting | bytes 7340032 | tf_op jit(solution)/shard_map/gather | solution.py:110
  289.5 9.1 %fusion.17 = bf16[4,128,3584]{2,0,1:T(4,128)(2,1)} fusion(bf16[128,4,3584]{2,1,0:T(4,128)(2,1)} %reshape.125, f32[128,4]{1,0:T(8,128)S(1)} %copy.57, s32[128,4]{1,0:T(8,128)S(1)} %copy.55, pred[128,4]{1,0:T(8,128)(4,1)S(1)} %copy.56), kind=kOutput, calls=%fused_computation.26 | convolution fusion | flops 89921536 | bytes 7344640 | tf_op jit(solution)/shard_map/tkg,tkd->gtd/dot_general | solution.py:112
  298.7 6.5 %reduce_sum.62 = bf16[128,3584]{1,0:T(8,128)(2,1)S(1)} reduce(bf16[4,128,3584]{2,0,1:T(4,128)(2,1)} %fusion.17, bf16[]{:T(256)} %constant.72.clone.1), dimensions={0}, to_apply=%region_4.5 | reduce | flops 1376256 | bytes 4587522 | tf_op jit(solution)/shard_map/reduce_sum | solution.py:62
  306.9 6.2 %gather_fusion.3 = f32[640,3584]{1,0:T(8,128)} fusion(f32[128,3584]{1,0:T(8,128)S(1)} %fusion.21, s32[1024]{0:T(1024)S(1)} %pad_clamp_fusion.2), kind=kCustom, calls=%fused_computation.3 | custom fusion | bytes 18352640 | tf_op jit(solution)/shard_map/gather | solution.py:119
  313.1 10.5 %gather.29 = f32[128,5,3584]{2,1,0:T(8,128)} reshape(f32[640,3584]{1,0:T(8,128)} %gather_fusion.3) | data formatting | bytes 18350080 | tf_op jit(solution)/shard_map/gather | solution.py:119
  323.7 10.3 %multiply_convert_fusion = bf16[128,5,3584]{2,1,0:T(8,128)(2,1)} fusion(f32[128,5,3584]{2,1,0:T(8,128)} %gather.29, f32[128,5]{1,0:T(8,128)S(1)} %mul.105), kind=kLoop, calls=%fused_computation.7 | loop fusion | flops 4587520 | bytes 13765120 | tf_op jit(solution)/shard_map/convert_element_type | solution.py:120
  334.0 94.1 %all_to_all.21 = bf16[128,5,3584]{2,1,0:T(8,128)(2,1)} all-to-all(bf16[128,5,3584]{2,1,0:T(8,128)(2,1)} %multiply_convert_fusion), channel_id=1, replica_groups=mesh['group'=4,'local'=32] {'group','local'}, dimensions={0} | all-to-all | bytes 9175040 | tf_op jit(solution)/shard_map/all_to_all | solution.py:123
  428.1 8.1 %reshape.113 = bf16[640,3584]{1,0:T(8,128)(2,1)} reshape(bf16[128,5,3584]{2,1,0:T(8,128)(2,1)} %all_to_all.21) | data formatting | bytes 9175040 | tf_op jit(solution)/shard_map/reshape | solution.py:32
  436.3 8.7 %fusion = f32[640,1024]{1,0:T(8,128)S(1)} fusion(bf16[640,3584]{1,0:T(8,128)(2,1)} %reshape.113, bf16[1,1024,3584]{2,1,0:T(8,128)(2,1)} %param.14), kind=kOutput, calls=%fused_computation.9 | convolution fusion | flops 4697620480 | bytes 14548992 | tf_op jit(solution)/shard_map/dot_general | solution.py:35
  446.5 10.5 %fusion.4 = f32[640,3584]{1,0:T(8,128)} fusion(bf16[1,3584,1024]{2,1,0:T(8,128)(2,1)} %param.13, f32[640,1024]{1,0:T(8,128)S(1)} %fusion, f32[640,1024]{1,0:T(8,128)S(1)} %copy-done.9), kind=kOutput, calls=%fused_computation.13 | convolution fusion | flops 4701552640 | bytes 21757952 | tf_op jit(solution)/shard_map/dot_general | solution.py:41
  457.0 15.5 %add_convert_fusion = bf16[640,3584]{1,0:T(8,128)(2,1)} fusion(f32[640,3584]{1,0:T(8,128)} %fusion.4, bf16[1,3584,1024]{2,1,0:T(8,128)(2,1)} %param.12, f32[640,1024]{1,0:T(8,128)} %copy-done.8, f32[640,1024]{1,0:T(8,128)} %copy-done.10, f32[640,1024]{1,0:T(8,128)} %copy-done.11), kind=kOutput, calls=%fused_computation.8 | convolution fusion | flops 4708761600 | bytes 28966912 | tf_op jit(solution)/shard_map/dot_general | solution.py:40
  472.5 7.8 %reshape.114 = bf16[128,5,3584]{2,1,0:T(8,128)(2,1)} reshape(bf16[640,3584]{1,0:T(8,128)(2,1)} %add_convert_fusion) | data formatting | bytes 9175040 | tf_op jit(solution)/shard_map/reshape | solution.py:44
  480.3 6.0 all-to-all-start.3
  491.1 81.8 %all-to-all-done.3 = bf16[128,5,3584]{2,1,0:T(8,128)(2,1)} async-done(((bf16[128,5,3584]{2,1,0:T(8,128)(2,1)}), bf16[128,5,3584]{2,1,0:T(8,128)(2,1)}, u32[]{:S(2)}, u32[]{:S(2)}) %all-to-all-start.3) | async-done | bytes 4587552 | tf_op jit(solution)/shard_map/all_to_all | solution.py:127
  572.9 8.1 %reshape.115 = bf16[640,3584]{1,0:T(8,128)(2,1)} reshape(bf16[128,5,3584]{2,1,0:T(8,128)(2,1)} %all-to-all-done.3) | data formatting | bytes 9175040 | tf_op jit(solution)/shard_map/reshape | solution.py:129
  581.0 10.8 %gather_fusion.4 = bf16[512,3584]{1,0:T(8,128)(2,1)} fusion(bf16[640,3584]{1,0:T(8,128)(2,1)} %reshape.115, s32[1024]{0:T(1024)S(1)} %pad_clamp_fusion.1), kind=kCustom, calls=%fused_computation.4 | custom fusion | bytes 7342080 | tf_op jit(solution)/shard_map/gather | solution.py:133
  591.8 7.2 %reshape.149 = bf16[128,4,3584]{2,1,0:T(4,128)(2,1)} reshape(bf16[512,3584]{1,0:T(8,128)(2,1)} %gather_fusion.4) | data formatting | bytes 7340032 | tf_op jit(solution)/shard_map/gather | solution.py:133
  599.0 5.9 fusion.18
  604.9 7.4 %reduce_sum.63 = bf16[128,3584]{1,0:T(8,128)(2,1)} reduce(bf16[4,128,3584]{2,0,1:T(4,128)(2,1)} %fusion.18, bf16[]{:T(256)} %constant.72.clone.1), dimensions={0}, to_apply=%region_5.6 | reduce | flops 1376256 | bytes 4587522 | tf_op jit(solution)/shard_map/reduce_sum | solution.py:62
  (71 shorter events, 28.0 us)
Async XLA Ops:
  2.6 3.8 copy-start.3
  2.6 3.9 copy-start.2
  2.6 7.4 %copy-start.5 = (f32[128,28]{0,1:T(8,128)S(1)}, f32[128,28]{0,1:T(8,128)}, u32[]{:S(2)}) copy-start(f32[128,28]{0,1:T(8,128)} %param.9) | copy-start | bytes 43012
  6.4 0.5 copy-start.6
  137.7 8.6 %copy-start = (bf16[640,3584]{1,0:T(8,128)(2,1)S(1)}, bf16[640,3584]{1,0:T(8,128)(2,1)}, u32[]{:S(2)}) copy-start(bf16[640,3584]{1,0:T(8,128)(2,1)} %reshape.109) | copy-start | bytes 13762564
  137.7 18.3 %slice-start = ((s8[7340032]{0:T(1024)(128)(4,1)}), s8[4194304]{0:T(1024)(128)(4,1)S(1)}, s32[]{:S(2)}) async-start(s8[7340032]{0:T(1024)(128)(4,1)} %bitcast.36), calls=%async_computation.4 | async-start | bytes 8388608
  146.4 8.1 %copy-start.8 = (f32[640,1024]{1,0:T(8,128)}, f32[640,1024]{1,0:T(8,128)S(1)}, u32[]{:S(2)}) copy-start(f32[640,1024]{1,0:T(8,128)S(1)} %fusion.10) | copy-start | bytes 7864324
  146.4 9.6 %slice-start.1 = ((s8[7340032]{0:T(1024)(128)(4,1)}), s8[3145728]{0:T(1024)(128)(4,1)S(1)}, s32[]{:S(2)}) async-start(s8[7340032]{0:T(1024)(128)(4,1)} %bitcast.36), calls=%async_computation.5 | async-start | bytes 6291456
  154.5 1.5 copy-start.11
  171.2 92.3 %all-to-all-start.1 = ((bf16[128,5,3584]{2,1,0:T(8,128)(2,1)}), bf16[128,5,3584]{2,1,0:T(8,128)(2,1)}, u32[]{:S(2)}, u32[]{:S(2)}) async-start(bf16[128,5,3584]{2,1,0:T(8,128)(2,1)} %reshape.110), calls=%async_computation.1 | async-start | bytes 14680064 | tf_op jit(solution)/shard_map/all_to_all | solution.py:106
  305.2 8.0 %copy-start.1 = (bf16[128,3584]{1,0:T(8,128)(2,1)}, bf16[128,3584]{1,0:T(8,128)(2,1)S(1)}, u32[]{:S(2)}) copy-start(bf16[128,3584]{1,0:T(8,128)(2,1)S(1)} %reduce_sum.62) | copy-start | bytes 2752516
  436.3 10.2 %copy-start.9 = (f32[640,1024]{1,0:T(8,128)S(1)}, f32[640,1024]{1,0:T(8,128)}, u32[]{:S(2)}) copy-start(f32[640,1024]{1,0:T(8,128)} %copy-done.8) | copy-start | bytes 7864324
  445.0 1.5 copy-start.10
  480.3 92.6 %all-to-all-start.3 = ((bf16[128,5,3584]{2,1,0:T(8,128)(2,1)}), bf16[128,5,3584]{2,1,0:T(8,128)(2,1)}, u32[]{:S(2)}, u32[]{:S(2)}) async-start(bf16[128,5,3584]{2,1,0:T(8,128)(2,1)} %reshape.114), calls=%async_computation.3 | async-start | bytes 14680064 | tf_op jit(solution)/shard_map/all_to_all | solution.py:127
  486.3 4.1 copy-start.4
  486.3 4.1 copy-start.7
where the time goes:
time: 624 us; the launch traced here: 612 us
  blocking collectives  192 us (31%)
  waiting for transfers between devices  163 us (26%)
  local copies, waits for them, and re-layouts  133 us (21%)
  matrix products  73.8 us (12%)
  other arithmetic  37.6 us (6%)
  starting transfers between devices  11.8 us (2%)
    all_to_all x1, blocking collectives, per_device(): lax.all_to_all(send_rows, ('group', 'local'), split_axis=0, concat_axis=0...  98.3 us
    all_to_all x1, blocking collectives, per_device(): lax.all_to_all(grad_send, ('group', 'local'), split_axis=0, concat_axis=0...  94.1 us
    all_to_all x1, waiting for transfers between devices, per_device(): lax.all_to_all(grad_rows, ('group', 'local'), split_axis=0, concat_axis=0...  81.8 us
    all_to_all x1, waiting for transfers between devices, per_device(): lax.all_to_all(stashed[0], ('group', 'local'), split_axis=0, concat_axis=...  81.2 us
    gather x2, local copies, waits for them, and re-layouts, per_device(): grad_ret[lookup].astype(jnp.float32)  17.9 us
    gather x2, local copies, waits for them, and re-layouts, per_device(): outputs = returned[lookup].astype(jnp.float32)  17.8 us
    gather x2, local copies, waits for them, and re-layouts, per_device(): upstream[token_pos]  16.7 us
    dot_general x1, matrix products, expert_back(): lax.dot_general(grad_gate, gate_mat, CONTRACT_LAST, preferred_element_typ...  15.5 us
  transfers between devices with their start and end apart: 2, of which 2 were waited for; matrix products, arithmetic and copies ran while one was open for 2% of the time, Pallas kernels for 0%

commit v1 on v0

v1 whole, which is shorter than its diff:
```python
import functools
import jax
import jax.numpy as jnp
from jax import lax
from jax.experimental import pallas as pl
from jax.experimental.pallas import tpu as pltpu
from jax.sharding import PartitionSpec as P

T = 128
E = 128
D = 3584
H = 1024
K = 4
CAP = 5
LANE = 128
NB = D // LANE
MAIN = 18
TAIL = NB - MAIN
ROWS = CAP * E
MSG_ROWS = 8 * E
MSG_COLS = MAIN * LANE
GP = 32
GR = GP * 8
F32 = jnp.float32
BF = jnp.bfloat16
NT = (((1,), (1,)), ((), ()))
VMEM_LIMIT = 56 * 1024 * 1024
CHUNKS = ((0, 6), (6, 6), (12, 6))


def cell_of(slot, block):
    index = slot * TAIL + block
    return 5 + index // MAIN, index % MAIN


CELLS = {cell_of(s, b): (s, b) for s in range(CAP) for b in range(TAIL)}


def iota(shape, dim):
    return lax.broadcasted_iota(jnp.int32, shape, dim)


def one_hot(cond):
    return jnp.where(cond, 1.0, 0.0).astype(BF)


def perm_unpack():
    r = iota((GR, GR), 0)
    return one_hot(iota((GR, GR), 1) == (r % GP) * 8 + r // GP)


def perm_pack():
    r = iota((GR, GR), 0)
    return one_hot(iota((GR, GR), 1) == (r % 8) * GP + r // 8)


def unpack(msg_ref, rows_ref):
    perm = perm_unpack()
    for g in range(E // GP):
        for first, count in CHUNKS:
            lanes = slice(first * LANE, (first + count) * LANE)
            moved = jnp.dot(perm, msg_ref[g * GR:(g + 1) * GR, lanes], preferred_element_type=F32).astype(BF)
            for s in range(CAP):
                rows_ref[s * E + g * GP:s * E + (g + 1) * GP, lanes] = moved[s * GP:(s + 1) * GP]
            for q in range(5, 8):
                for c in range(first, first + count):
                    if (q, c) in CELLS:
                        s, b = CELLS[q, c]
                        rows_ref[s * E + g * GP:s * E + (g + 1) * GP, (MAIN + b) * LANE:(MAIN + b + 1) * LANE] = (
                            moved[q * GP:(q + 1) * GP, (c - first) * LANE:(c - first + 1) * LANE]
                        )


def pack(rows_ref, msg_ref):
    perm = perm_pack()
    blank = jnp.zeros((GP, LANE), BF)
    for g in range(E // GP):
        for first, count in CHUNKS:
            lanes = slice(first * LANE, (first + count) * LANE)
            parts = [rows_ref[s * E + g * GP:s * E + (g + 1) * GP, lanes] for s in range(CAP)]
            for q in range(5, 8):
                cells = []
                for c in range(first, first + count):
                    if (q, c) in CELLS:
                        s, b = CELLS[q, c]
                        cells.append(rows_ref[s * E + g * GP:s * E + (g + 1) * GP, (MAIN + b) * LANE:(MAIN + b + 1) * LANE])
                    else:
                        cells.append(blank)
                parts.append(jnp.concatenate(cells, axis=1))
            stacked = jnp.concatenate(parts, axis=0)
            msg_ref[g * GR:(g + 1) * GR, lanes] = jnp.dot(perm, stacked, preferred_element_type=F32).astype(BF)


def slots_of(ids):
    expert = iota((E, T), 0)
    hits = [jnp.where(ids[k:k + 1, :] == expert, 1.0, 0.0) for k in range(K)]
    hit = hits[0] + hits[1] + hits[2] + hits[3]
    earlier = one_hot(iota((T, T), 0) < iota((T, T), 1))
    before = jnp.dot(hit.astype(BF), earlier, preferred_element_type=F32)
    return hits, hit, before


def gates_of(scores):
    sigma = jax.nn.sigmoid(scores)
    total = jnp.sum(sigma, axis=0, keepdims=True)
    return sigma, total


def dispatch_kernel(ids_ref, scales_ref, codes_ref, msg_ref, square, tokens, rows):
    _, hit, before = slots_of(ids_ref[...])
    square[...] = jnp.zeros((LANE, T), F32)
    square[0:NB, :] = scales_ref[...]
    scale = square[...].T
    for j in range(NB):
        lanes = slice(j * LANE, (j + 1) * LANE)
        tokens[:, lanes] = (codes_ref[:, lanes].astype(F32) * scale[:, j:j + 1]).astype(BF)
    for s in range(CAP):
        pick = one_hot((hit > 0.5) & (before == float(s)))
        for n in range(0, D, 512):
            rows[s * E:(s + 1) * E, n:n + 512] = jnp.dot(pick, tokens[:, n:n + 512], preferred_element_type=F32).astype(BF)
    pack(rows, msg_ref)


def table_kernel(ids_ref, scores_ref, spread_ref, mix_ref, sum_ref):
    ids = ids_ref[...]
    hits, hit, before = slots_of(ids)
    sigma, total = gates_of(scores_ref[...])
    weight = (2.5 * sigma / total).astype(BF).astype(F32)
    weighted = hits[0] * weight[0:1]
    for k in range(1, K):
        weighted = weighted + hits[k] * weight[k:k + 1]
    for s in range(CAP):
        here = (hit > 0.5) & (before == float(s))
        spread = jnp.where(here, weighted, 0.0)
        spread_ref[s * E:(s + 1) * E, :] = spread.astype(BF)
        mix_ref[:, s * E:(s + 1) * E] = spread.T.astype(BF)
        sum_ref[:, s * E:(s + 1) * E] = jnp.where(here, 1.0, 0.0).T.astype(BF)


def forward_kernel(msg_ref, gate_ref, up_ref, down_ref, out_ref, pre_gate_ref, pre_up_ref, rows, active):
    step = pl.program_id(0)

    @pl.when(step == 0)
    def _():
        unpack(msg_ref, rows)

    @pl.when(step < 4)
    def _():
        pre_gate = jnp.dot(rows[...], gate_ref[...], preferred_element_type=F32)
        pre_up = jnp.dot(rows[...], up_ref[...], preferred_element_type=F32)
        pre_gate_ref[...] = pre_gate
        pre_up_ref[...] = pre_up
        at = pl.multiple_of(step * 256, 256)
        active[:, pl.ds(at, 256)] = (pre_gate * jax.nn.sigmoid(pre_gate) * pre_up).astype(BF)

    @pl.when(step >= 4)
    def _():
        at = pl.multiple_of((step - 4) * 512, 512)
        rows[:, pl.ds(at, 512)] = jnp.dot(active[...], down_ref[...], preferred_element_type=F32).astype(BF)

    @pl.when(step == 10)
    def _():
        pack(rows, out_ref)


def backward_kernel(msg_ref, pre_gate_ref, pre_up_ref, gate_ref, up_ref, down_ref, out_ref, rows, d_gate, d_up):
    step = pl.program_id(0)

    @pl.when(step == 0)
    def _():
        unpack(msg_ref, rows)

    @pl.when(step < 4)
    def _():
        grad_act = lax.dot_general(rows[...], down_ref[...], NT, preferred_element_type=F32)
        pre_gate = pre_gate_ref[...]
        sig = jax.nn.sigmoid(pre_gate)
        at = pl.multiple_of(step * 256, 256)
        d_up[:, pl.ds(at, 256)] = (grad_act * (pre_gate * sig)).astype(BF)
        d_gate[:, pl.ds(at, 256)] = (grad_act * pre_up_ref[...] * (sig * (1.0 + pre_gate * (1.0 - sig)))).astype(BF)

    @pl.when(step >= 4)
    def _():
        at = pl.multiple_of((step - 4) * 512, 512)
        summed = lax.dot_general(d_gate[...], gate_ref[...], NT, preferred_element_type=F32)
        summed = summed + lax.dot_general(d_up[...], up_ref[...], NT, preferred_element_type=F32)
        rows[:, pl.ds(at, 512)] = summed.astype(BF)

    @pl.when(step == 10)
    def _():
        pack(rows, out_ref)


def combine_kernel(msg_ref, mix_ref, spread_ref, teacher_ref, student_ref, upstream_ref, out_ref, rows):
    unpack(msg_ref, rows)
    for n in range(0, D, 512):
        lanes = slice(n, n + 512)
        student = jnp.dot(mix_ref[...], rows[:, lanes], preferred_element_type=F32).astype(BF)
        student_ref[:, lanes] = student
        upstream = (student.astype(F32) - teacher_ref[:, lanes].astype(F32)).astype(BF)
        upstream_ref[:, lanes] = upstream
    for n in range(0, D, 512):
        lanes = slice(n, n + 512)
        rows[:, lanes] = jnp.dot(spread_ref[...], upstream_ref[:, lanes], preferred_element_type=F32).astype(BF)
    pack(rows, out_ref)


def score_kernel(msg_ref, upstream_ref, ids_ref, scores_ref, out_ref, rows):
    unpack(msg_ref, rows)
    inner = lax.dot_general(rows[...], upstream_ref[...], NT, preferred_element_type=F32)
    hits, hit, before = slots_of(ids_ref[...])
    by_expert = jnp.zeros((E, T), F32)
    for s in range(CAP):
        here = (hit > 0.5) & (before == float(s))
        by_expert = by_expert + jnp.where(here, inner[s * E:(s + 1) * E], 0.0)
    grad_w = jnp.concatenate([jnp.sum(hits[k] * by_expert, axis=0, keepdims=True) for k in range(K)], axis=0)
    sigma, total = gates_of(scores_ref[...])
    inner_sum = jnp.sum(grad_w * sigma, axis=0, keepdims=True)
    out_ref[...] = 2.5 * sigma * (1.0 - sigma) * (grad_w / total - inner_sum / (total * total))


def gather_kernel(msg_ref, sum_ref, out_ref, rows):
    unpack(msg_ref, rows)
    for n in range(0, D, 512):
        lanes = slice(n, n + 512)
        out_ref[:, lanes] = jnp.dot(sum_ref[...], rows[:, lanes], preferred_element_type=F32).astype(BF)


def struct(shape, dtype):
    return jax.ShapeDtypeStruct(shape, dtype)


PARAMS = pltpu.CompilerParams(vmem_limit_bytes=VMEM_LIMIT)
ROWS_SCRATCH = pltpu.VMEM((ROWS, D), BF)
MSG = struct((MSG_ROWS, MSG_COLS), BF)


def cost(flops, moved):
    return pl.CostEstimate(flops=flops, bytes_accessed=moved, transcendentals=0)


def dispatch(ids, scales, codes):
    return pl.pallas_call(
        dispatch_kernel, out_shape=MSG, name="dispatch",
        scratch_shapes=[pltpu.VMEM((LANE, T), F32), pltpu.VMEM((T, D), BF), ROWS_SCRATCH],
        compiler_params=PARAMS, cost_estimate=cost(2 * 10**9, 6 * 10**6),
    )(ids, scales, codes)


def tables(ids, scores):
    return pl.pallas_call(
        table_kernel, name="tables",
        out_shape=(struct((ROWS, T), BF), struct((T, ROWS), BF), struct((T, ROWS), BF)),
        compiler_params=PARAMS, cost_estimate=cost(10**8, 5 * 10**5),
    )(ids, scores)


def whole(shape):
    return pl.BlockSpec(shape, lambda i: (0, 0), pipeline_mode=pl.Buffered(1))


def forward(msg, gate, up, down):
    return pl.pallas_call(
        forward_kernel, name="expert_forward",
        grid=(11,),
        in_specs=[
            whole((MSG_ROWS, MSG_COLS)),
            pl.BlockSpec((D, 256), lambda i: (0, jnp.minimum(i, 3))),
            pl.BlockSpec((D, 256), lambda i: (0, jnp.minimum(i, 3))),
            pl.BlockSpec((H, 512), lambda i: (0, jnp.maximum(i - 4, 0))),
        ],
        out_specs=(
            whole((MSG_ROWS, MSG_COLS)),
            pl.BlockSpec((ROWS, 256), lambda i: (0, jnp.minimum(i, 3))),
            pl.BlockSpec((ROWS, 256), lambda i: (0, jnp.minimum(i, 3))),
        ),
        out_shape=(MSG, struct((ROWS, H), F32), struct((ROWS, H), F32)),
        scratch_shapes=[ROWS_SCRATCH, pltpu.VMEM((ROWS, H), BF)],
        compiler_params=PARAMS, cost_estimate=cost(15 * 10**9, 37 * 10**6),
    )(msg, gate, up, down)


def backward(msg, pre_gate, pre_up, gate, up, down):
    return pl.pallas_call(
        backward_kernel, name="expert_backward",
        grid=(11,),
        in_specs=[
            whole((MSG_ROWS, MSG_COLS)),
            pl.BlockSpec((ROWS, 256), lambda i: (0, jnp.minimum(i, 3))),
            pl.BlockSpec((ROWS, 256), lambda i: (0, jnp.minimum(i, 3))),
            pl.BlockSpec((512, H), lambda i: (jnp.maximum(i - 4, 0), 0)),
            pl.BlockSpec((512, H), lambda i: (jnp.maximum(i - 4, 0), 0)),
            pl.BlockSpec((256, D), lambda i: (jnp.minimum(i, 3), 0)),
        ],
        out_specs=whole((MSG_ROWS, MSG_COLS)),
        out_shape=MSG,
        scratch_shapes=[ROWS_SCRATCH, pltpu.VMEM((ROWS, H), BF), pltpu.VMEM((ROWS, H), BF)],
        compiler_params=PARAMS, cost_estimate=cost(15 * 10**9, 37 * 10**6),
    )(msg, pre_gate, pre_up, gate, up, down)


def combine(msg, mix, spread, teacher):
    return pl.pallas_call(
        combine_kernel, name="combine",
        out_shape=(struct((T, D), BF), struct((T, D), BF), MSG),
        scratch_shapes=[ROWS_SCRATCH],
        compiler_params=PARAMS, cost_estimate=cost(3 * 10**9, 12 * 10**6),
    )(msg, mix, spread, teacher)


def scores_grad(msg, upstream, ids, scores):
    return pl.pallas_call(
        score_kernel, name="scores_grad",
        out_shape=struct((K, T), F32),
        scratch_shapes=[ROWS_SCRATCH],
        compiler_params=PARAMS, cost_estimate=cost(2 * 10**9, 6 * 10**6),
    )(msg, upstream, ids, scores)


def gather(msg, sums):
    return pl.pallas_call(
        gather_kernel, name="gather_tokens",
        out_shape=struct((T, D), BF),
        scratch_shapes=[ROWS_SCRATCH],
        compiler_params=PARAMS, cost_estimate=cost(2 * 10**9, 6 * 10**6),
    )(msg, sums)


def exchange(msg):
    return lax.all_to_all(msg, ("group", "local"), split_axis=0, concat_axis=0, tiled=True)


def per_device(token_codes, block_scales, route_scores, expert_ids, w_gate, w_up, w_down, teacher):
    ids = expert_ids.T
    scores = route_scores.T
    gate, up, down = w_gate[0], w_up[0], w_down[0]
    arrived = exchange(dispatch(ids, block_scales.T, token_codes))
    spread, mix, sums = tables(ids, scores)
    out_msg, pre_gate, pre_up = forward(arrived, gate, up, down)
    returned = exchange(out_msg)
    student_out, upstream, grad_msg = combine(returned, mix, spread, teacher)
    grad_in = exchange(grad_msg)
    grad_scores = scores_grad(returned, upstream, ids, scores)
    grad_back = exchange(backward(grad_in, pre_gate, pre_up, gate, up, down))
    grad_tokens = gather(grad_back, sums)
    return student_out, grad_tokens, grad_scores.T


def solution(mesh):
    rows = P(("group", "local"), None)
    mats = P(("group", "local"), None, None)
    return jax.shard_map(
        per_device, mesh=mesh, in_specs=(rows, rows, rows, rows, mats, mats, mats, rows),
        out_specs=(rows, rows, rows), check_vma=False,
    )
```

time: 624 us -> 340 us (0.54); the launches traced: 612 us -> 340 us
  local copies, waits for them, and re-layouts: 133 us -> 0 us
  Pallas kernels: 0 us -> 84.3 us
  matrix products: 73.8 us -> 0 us
  blocking collectives: 192 us -> 134 us
  waiting for transfers between devices: 163 us -> 110 us
  other arithmetic: 37.6 us -> 0 us
    pallas_call x0 -> x7, Pallas kernels: none -> 84.3 us  [the longest x1 28.1 us: forward(): pl.pallas_call(forward_kernel, name='expert_forward', grid=(11,), in_spec...]
    dot_general x8 -> x0, matrix products: 73.8 us -> none  [the longest x1 15.5 us: expert_back(): lax.dot_general(grad_gate, gate_mat, CONTRACT_LAST, preferred_element_typ...]
    gather x14 -> x0, local copies, waits for them, and re-layouts: 73.8 us -> none  [the longest x2 17.9 us: per_device(): grad_ret[lookup].astype(jnp.float32)]
    all_to_all x2, blocking collectives: 192 us -> 134 us  [exchange(): lax.all_to_all(msg, ('group', 'local'), split_axis=0, concat_axis=0, tile...]
    all_to_all x2, waiting for transfers between devices: 163 us -> 110 us  [exchange(): lax.all_to_all(msg, ('group', 'local'), split_axis=0, concat_axis=0, tile...]
    reshape x8 -> x0, local copies, waits for them, and re-layouts: 48.4 us -> none  [the longest x1 8.14 us: expert_pre(): flat_rows = in_rows.reshape(-1, in_rows.shape[-1])]
    reduce_sum x6 -> x0, other arithmetic: 18.8 us -> none  [the longest x2 13.9 us: group_sum(): jnp.sum(group_parts.astype(jnp.float32), axis=axis_num).astype(jnp.bfloat16)]
    convert_element_type x3 -> x0, other arithmetic: 13.4 us -> none  [the longest x1 10.3 us: per_device(): grad_send = (slot_scale[:, None] * upstream[token_pos]).astype(jnp.bfloat...]
  transfers between devices with their start and end apart: 2 -> 2, of which waited for: 2 -> 2; matrix products, arithmetic and copies ran while one was open for 2% -> 0% of each run, Pallas kernels for 0% -> 2%
where the time goes in v1:
time: 340 us
  blocking collectives  134 us (39%)
  waiting for transfers between devices  110 us (32%)
  Pallas kernels  84.3 us (25%)
  starting transfers between devices  11.2 us (3%)
    all_to_all x2, blocking collectives, exchange(): lax.all_to_all(msg, ('group', 'local'), split_axis=0, concat_axis=0, tile...  134 us
    all_to_all x2, waiting for transfers between devices, exchange(): lax.all_to_all(msg, ('group', 'local'), split_axis=0, concat_axis=0, tile...  110 us
    pallas_call x1, Pallas kernels, forward(): pl.pallas_call(forward_kernel, name='expert_forward', grid=(11,), in_spec...  28.1 us
    pallas_call x1, Pallas kernels, backward(): pl.pallas_call(backward_kernel, name='expert_backward', grid=(11,), in_sp...  26.8 us
    all_to_all x2, starting transfers between devices, exchange(): lax.all_to_all(msg, ('group', 'local'), split_axis=0, concat_axis=0, tile...  11.2 us
    pallas_call x1, Pallas kernels, combine(): pl.pallas_call(combine_kernel, name='combine', out_shape=(struct((T, D),...  9.55 us
    pallas_call x1, Pallas kernels, dispatch(): pl.pallas_call(dispatch_kernel, out_shape=MSG, name='dispatch', scratch_s...  6.82 us
  transfers between devices with their start and end apart: 2, of which 2 were waited for; matrix products, arithmetic and copies ran while one was open for 0% of the time, Pallas kernels for 2%

profile of v1, /device:TPU:1, one launch (start us, length us, event | category | flops | bytes accessed | tf_op | source)
XLA Modules:
  0.0 339.6 jit_solution(238328704066568206)
XLA Ops:
  0.6 6.8 %dispatch.1 = bf16[1024,2304]{1,0:T(8,128)(2,1)} custom-call(s32[4,128]{1,0:T(4,128)} %bitcast.28, f32[28,128]{1,0:T(8,128)} %bitcast.27, bf16[128,3584]{1,0:T(8,128)(2,1)} %codes_ref.1), custom_call_target="tpu_custom_call" | custom-call | flops 2000000000 | bytes 6000000 | tf_op jit(solution)/shard_map/dispatch/pallas_call | solution.py:243
  7.5 70.1 %all_to_all.44 = bf16[128,8,2304]{2,1,0:T(8,128)(2,1)} all-to-all(bf16[128,8,2304]{2,1,0:T(8,128)(2,1)} %bitcast.20), channel_id=1, replica_groups=mesh['group'=4,'local'=32] {'group','local'}, dimensions={0} | all-to-all | bytes 9437184 | tf_op jit(solution)/shard_map/all_to_all | solution.py:330
  77.5 28.1 %expert_forward.1 = (bf16[1024,2304]{1,0:T(8,128)(2,1)}, f32[640,1024]{1,0:T(8,128)}, f32[640,1024]{1,0:T(8,128)}) custom-call(bf16[1024,2304]{1,0:T(8,128)(2,1)} %bitcast.18, bf16[3584,1024]{1,0:T(8,128)(2,1)} %bitcast.21, bf16[3584,1024]{1,0:T(8,128)(2,1)} %bitcast.23, bf16[1024,3584]{1,0:T(8,128)(2,1)} %bitcast.25), custom_call_target="tpu_custom_call" | custom-call | flops 15000000512 | bytes 37000000 | tf_op jit(solution)/shard_map/expert_forward/pallas_call | solution.py:263
  105.6 5.6 %all-to-all-start.1 = ((bf16[128,8,2304]{2,1,0:T(8,128)(2,1)}), bf16[128,8,2304]{2,1,0:T(8,128)(2,1)}, u32[]{:S(2)}, u32[]{:S(2)}) async-start(bf16[128,8,2304]{2,1,0:T(8,128)(2,1)} %bitcast.15), calls=%async_computation.1 | async-start | bytes 9437184 | tf_op jit(solution)/shard_map/all_to_all | solution.py:330
  111.2 1.8 tables.1
  113.0 56.8 %all-to-all-done.1 = bf16[128,8,2304]{2,1,0:T(8,128)(2,1)} async-done(((bf16[128,8,2304]{2,1,0:T(8,128)(2,1)}), bf16[128,8,2304]{2,1,0:T(8,128)(2,1)}, u32[]{:S(2)}, u32[]{:S(2)}) %all-to-all-start.1) | async-done | bytes 4718624 | tf_op jit(solution)/shard_map/all_to_all | solution.py:330
  169.8 9.6 %combine.1 = (bf16[128,3584]{1,0:T(8,128)(2,1)}, bf16[128,3584]{1,0:T(8,128)(2,1)}, bf16[1024,2304]{1,0:T(8,128)(2,1)}) custom-call(bf16[1024,2304]{1,0:T(8,128)(2,1)} %bitcast.8.msg_ref, bf16[128,640]{1,0:T(8,128)(2,1)} %get-tuple-element.13.mix_ref, bf16[640,128]{1,0:T(8,128)(2,1)} %get-tuple-element.14.spread_ref, bf16[128,3584]{1,0:T(8,128)(2,1)} %teacher_ref.1), custom_call_target="tpu_custom_call" | custom-call | flops 3000000000 | bytes 12000000 | tf_op jit(solution)/shard_map/combine/pallas_call | solution.py:303
  179.3 63.9 %all_to_all.45 = bf16[128,8,2304]{2,1,0:T(8,128)(2,1)} all-to-all(bf16[128,8,2304]{2,1,0:T(8,128)(2,1)} %bitcast.17), channel_id=1, replica_groups=mesh['group'=4,'local'=32] {'group','local'}, dimensions={0} | all-to-all | bytes 9437184 | tf_op jit(solution)/shard_map/all_to_all | solution.py:330
  243.2 26.8 %expert_backward.1 = bf16[1024,2304]{1,0:T(8,128)(2,1)} custom-call(bf16[1024,2304]{1,0:T(8,128)(2,1)} %bitcast.19, f32[640,1024]{1,0:T(8,128)} %get-tuple-element.17.pre_gate_ref, f32[640,1024]{1,0:T(8,128)} %get-tuple-element.18.pre_up_ref, bf16[3584,1024]{1,0:T(8,128)(2,1)} %bitcast.22, bf16[3584,1024]{1,0:T(8,128)(2,1)} %bitcast.24, ...), custom_call_target="tpu_custom_call" | custom-call | flops 15000000512 | bytes 37000000 | tf_op jit(solution)/shard_map/expert_backward/pallas_call | solution.py:284
  270.0 5.6 %all-to-all-start.3 = ((bf16[128,8,2304]{2,1,0:T(8,128)(2,1)}), bf16[128,8,2304]{2,1,0:T(8,128)(2,1)}, u32[]{:S(2)}, u32[]{:S(2)}) async-start(bf16[128,8,2304]{2,1,0:T(8,128)(2,1)} %bitcast.16), calls=%async_computation.3 | async-start | bytes 9437184 | tf_op jit(solution)/shard_map/all_to_all | solution.py:330
  275.6 5.9 %scores_grad.1 = f32[4,128]{1,0:T(4,128)} custom-call(bf16[1024,2304]{1,0:T(8,128)(2,1)} %bitcast.8.msg_ref, bf16[128,3584]{1,0:T(8,128)(2,1)} %get-tuple-element.20.upstream_ref, s32[4,128]{1,0:T(4,128)} %bitcast.30, f32[4,128]{1,0:T(4,128)} %bitcast.32), custom_call_target="tpu_custom_call" | custom-call | flops 2000000000 | bytes 6000000 | tf_op jit(solution)/shard_map/scores_grad/pallas_call | solution.py:312
  281.5 52.7 %all-to-all-done.3 = bf16[128,8,2304]{2,1,0:T(8,128)(2,1)} async-done(((bf16[128,8,2304]{2,1,0:T(8,128)(2,1)}), bf16[128,8,2304]{2,1,0:T(8,128)(2,1)}, u32[]{:S(2)}, u32[]{:S(2)}) %all-to-all-start.3) | async-done | bytes 4718624 | tf_op jit(solution)/shard_map/all_to_all | solution.py:330
  334.3 5.4 %gather_tokens.1 = bf16[128,3584]{1,0:T(8,128)(2,1)} custom-call(bf16[1024,2304]{1,0:T(8,128)(2,1)} %bitcast.13.msg_ref, bf16[128,640]{1,0:T(8,128)(2,1)} %get-tuple-element.19.sum_ref), custom_call_target="tpu_custom_call" | custom-call | flops 2000000000 | bytes 6000000 | tf_op jit(solution)/shard_map/gather_tokens/pallas_call | solution.py:321
Async XLA Ops:
  105.6 64.2 %all-to-all-start.1 = ((bf16[128,8,2304]{2,1,0:T(8,128)(2,1)}), bf16[128,8,2304]{2,1,0:T(8,128)(2,1)}, u32[]{:S(2)}, u32[]{:S(2)}) async-start(bf16[128,8,2304]{2,1,0:T(8,128)(2,1)} %bitcast.15), calls=%async_computation.1 | async-start | bytes 9437184 | tf_op jit(solution)/shard_map/all_to_all | solution.py:330
  270.0 64.2 %all-to-all-start.3 = ((bf16[128,8,2304]{2,1,0:T(8,128)(2,1)}), bf16[128,8,2304]{2,1,0:T(8,128)(2,1)}, u32[]{:S(2)}, u32[]{:S(2)}) async-start(bf16[128,8,2304]{2,1,0:T(8,128)(2,1)} %bitcast.16), calls=%async_computation.3 | async-start | bytes 9437184 | tf_op jit(solution)/shard_map/all_to_all | solution.py:330

commit v2 on v1

v2 whole, which is shorter than its diff:
```python
import jax
import jax.numpy as jnp
from jax import lax
from jax.experimental import pallas as pl
from jax.experimental.pallas import tpu as pltpu
from jax.sharding import PartitionSpec as P

T = 128
E = 128
D = 3584
H = 1024
K = 4
CAP = 5
LANE = 128
NB = D // LANE
MAIN = 18
TAIL = NB - MAIN
ROWS = CAP * E
MSG_ROWS = 8 * E
MSG_COLS = MAIN * LANE
GP = 32
GR = GP * 8
F32 = jnp.float32
BF = jnp.bfloat16
NT = (((1,), (1,)), ((), ()))
VMEM_LIMIT = 56 * 1024 * 1024
CHUNKS = ((0, 6), (6, 6), (12, 6))
REST = (MAIN, TAIL)
TILES = (REST,) + CHUNKS


def lanes_of(chunk):
    return slice(chunk[0] * LANE, (chunk[0] + chunk[1]) * LANE)


def cell_of(slot, block):
    index = slot * TAIL + block
    return 5 + index // MAIN, index % MAIN


CELLS = {cell_of(s, b): (s, b) for s in range(CAP) for b in range(TAIL)}


def iota(shape, dim):
    return lax.broadcasted_iota(jnp.int32, shape, dim)


def one_hot(cond):
    return jnp.where(cond, 1.0, 0.0).astype(BF)


def perm_unpack():
    r = iota((GR, GR), 0)
    return one_hot(iota((GR, GR), 1) == (r % GP) * 8 + r // GP)


def perm_pack():
    r = iota((GR, GR), 0)
    return one_hot(iota((GR, GR), 1) == (r % 8) * GP + r // 8)


def unpack(msg_ref, rows_ref, perm, chunk):
    first, count = chunk
    lanes = lanes_of(chunk)
    for g in range(E // GP):
        moved = jnp.dot(perm, msg_ref[g * GR:(g + 1) * GR, lanes], preferred_element_type=F32).astype(BF)
        for s in range(CAP):
            rows_ref[s * E + g * GP:s * E + (g + 1) * GP, lanes] = moved[s * GP:(s + 1) * GP]
        for q in range(5, 8):
            for c in range(first, first + count):
                if (q, c) in CELLS:
                    s, b = CELLS[q, c]
                    rows_ref[s * E + g * GP:s * E + (g + 1) * GP, lanes_of((MAIN + b, 1))] = (
                        moved[q * GP:(q + 1) * GP, lanes_of((c - first, 1))]
                    )


def pack(rows_ref, msg_ref, perm, chunk):
    first, count = chunk
    lanes = lanes_of(chunk)
    blank = jnp.zeros((GP, LANE), BF)
    for g in range(E // GP):
        parts = [rows_ref[s * E + g * GP:s * E + (g + 1) * GP, lanes] for s in range(CAP)]
        for q in range(5, 8):
            cells = []
            for c in range(first, first + count):
                if (q, c) in CELLS:
                    s, b = CELLS[q, c]
                    cells.append(rows_ref[s * E + g * GP:s * E + (g + 1) * GP, lanes_of((MAIN + b, 1))])
                else:
                    cells.append(blank)
            parts.append(jnp.concatenate(cells, axis=1))
        stacked = jnp.concatenate(parts, axis=0)
        msg_ref[g * GR:(g + 1) * GR, lanes] = jnp.dot(perm, stacked, preferred_element_type=F32).astype(BF)


class Copies:
    def __init__(self, sems):
        self.sems = sems
        self.used = 0

    def start(self, source, target):
        copy = pltpu.make_async_copy(source, target, self.sems.at[self.used])
        self.used += 1
        copy.start()
        return copy


def wait_all(copies):
    for copy in copies:
        copy.wait()


def slots_of(ids):
    expert = iota((E, T), 0)
    hits = [jnp.where(ids[k:k + 1, :] == expert, 1.0, 0.0) for k in range(K)]
    hit = hits[0] + hits[1] + hits[2] + hits[3]
    earlier = one_hot(iota((T, T), 0) < iota((T, T), 1))
    before = jnp.dot(hit.astype(BF), earlier, preferred_element_type=F32)
    return hits, hit, before


def gates_of(scores):
    sigma = jax.nn.sigmoid(scores)
    total = jnp.sum(sigma, axis=0, keepdims=True)
    return sigma, total


def dispatch_kernel(ids_hbm, scales_hbm, codes_hbm, out_hbm, ids, scales, codes, tokens, rows, msg, sems):
    copies = Copies(sems)
    ids_copy = copies.start(ids_hbm, ids)
    scales_copy = copies.start(scales_hbm, scales.at[0:NB, :])
    code_copies = [copies.start(codes_hbm.at[:, lanes_of(t)], codes.at[:, lanes_of(t)]) for t in TILES]
    perm = perm_pack()
    ids_copy.wait()
    _, hit, before = slots_of(ids[...])
    picks = [one_hot((hit > 0.5) & (before == float(s))) for s in range(CAP)]
    pick = jnp.concatenate(picks, axis=0)
    scales_copy.wait()
    scale = scales[...].T
    sent = []
    for tile, copy in zip(TILES, code_copies):
        copy.wait()
        for j in range(tile[0], tile[0] + tile[1]):
            lanes = lanes_of((j, 1))
            tokens[:, lanes] = (codes[:, lanes].astype(F32) * scale[:, j:j + 1]).astype(BF)
        lanes = lanes_of(tile)
        rows[:, lanes] = jnp.dot(pick, tokens[:, lanes], preferred_element_type=F32).astype(BF)
        if tile is not REST:
            pack(rows, msg, perm, tile)
            sent.append(copies.start(msg.at[:, lanes], out_hbm.at[:, lanes]))
    wait_all(sent)


def table_kernel(ids_ref, scores_ref, spread_ref, mix_ref, sum_ref):
    ids = ids_ref[...]
    hits, hit, before = slots_of(ids)
    sigma, total = gates_of(scores_ref[...])
    weight = (2.5 * sigma / total).astype(BF).astype(F32)
    weighted = hits[0] * weight[0:1]
    for k in range(1, K):
        weighted = weighted + hits[k] * weight[k:k + 1]
    for s in range(CAP):
        here = (hit > 0.5) & (before == float(s))
        spread = jnp.where(here, weighted, 0.0)
        spread_ref[s * E:(s + 1) * E, :] = spread.astype(BF)
        mix_ref[:, s * E:(s + 1) * E] = spread.T.astype(BF)
        sum_ref[:, s * E:(s + 1) * E] = jnp.where(here, 1.0, 0.0).T.astype(BF)


def forward_kernel(
    msg_hbm, gate_hbm, up_hbm, down_hbm, out_hbm, pre_gate_hbm, pre_up_hbm,
    msg, rows, gate, up, down, active, pre_gate_all, pre_up_all, out, sems,
):
    copies = Copies(sems)
    quarter = [slice(n * 256, (n + 1) * 256) for n in range(4)]

    def fetch(n):
        return [
            copies.start(gate_hbm.at[:, quarter[n]], gate.at[:, quarter[n]]),
            copies.start(up_hbm.at[:, quarter[n]], up.at[:, quarter[n]]),
        ]

    def fetch_down(t):
        return [copies.start(down_hbm.at[:, lanes_of(t)], down.at[:, lanes_of(t)])]

    arriving = [copies.start(msg_hbm.at[:, lanes_of(c)], msg.at[:, lanes_of(c)]) for c in CHUNKS]
    coming = [fetch(0)]
    perm = perm_unpack()
    for chunk, copy in zip(CHUNKS, arriving):
        copy.wait()
        unpack(msg, rows, perm, chunk)
        if chunk is CHUNKS[0]:
            coming.append(fetch(1))
    sent = []
    coming_down = []
    for n in range(4):
        wait_all(coming[n])
        if n < 2:
            coming.append(fetch(n + 2))
        else:
            coming_down.extend([fetch_down(TILES[2 * n - 4]), fetch_down(TILES[2 * n - 3])])
        pre_gate = jnp.dot(rows[...], gate[:, quarter[n]], preferred_element_type=F32)
        pre_gate_all[:, quarter[n]] = pre_gate
        pre_up = jnp.dot(rows[...], up[:, quarter[n]], preferred_element_type=F32)
        pre_up_all[:, quarter[n]] = pre_up
        active[:, quarter[n]] = (pre_gate * jax.nn.sigmoid(pre_gate) * pre_up).astype(BF)
        sent.append(copies.start(pre_gate_all.at[:, quarter[n]], pre_gate_hbm.at[:, quarter[n]]))
        sent.append(copies.start(pre_up_all.at[:, quarter[n]], pre_up_hbm.at[:, quarter[n]]))
    perm = perm_pack()
    for tile, coming in zip(TILES, coming_down):
        wait_all(coming)
        lanes = lanes_of(tile)
        rows[:, lanes] = jnp.dot(active[...], down[:, lanes], preferred_element_type=F32).astype(BF)
        if tile is not REST:
            pack(rows, out, perm, tile)
            sent.append(copies.start(out.at[:, lanes], out_hbm.at[:, lanes]))
    wait_all(sent)


def backward_kernel(
    msg_hbm, pre_gate_hbm, pre_up_hbm, gate_hbm, up_hbm, down_hbm, out_hbm,
    msg, rows, both, down, pre_gate_all, pre_up_all, d_both, out, sems,
):
    copies = Copies(sems)
    quarter = [slice(n * 256, (n + 1) * 256) for n in range(4)]

    def fetch(n):
        return [
            copies.start(down_hbm.at[quarter[n], :], down.at[quarter[n], :]),
            copies.start(pre_gate_hbm.at[:, quarter[n]], pre_gate_all.at[:, quarter[n]]),
            copies.start(pre_up_hbm.at[:, quarter[n]], pre_up_all.at[:, quarter[n]]),
        ]

    def fetch_both(t):
        return [
            copies.start(gate_hbm.at[lanes_of(t), :], both.at[lanes_of(t), 0:H]),
            copies.start(up_hbm.at[lanes_of(t), :], both.at[lanes_of(t), H:2 * H]),
        ]

    arriving = [copies.start(msg_hbm.at[:, lanes_of(c)], msg.at[:, lanes_of(c)]) for c in CHUNKS]
    coming = [fetch(0)]
    perm = perm_unpack()
    for chunk, copy in zip(CHUNKS, arriving):
        copy.wait()
        unpack(msg, rows, perm, chunk)
        if chunk is CHUNKS[0]:
            coming.append(fetch(1))
    coming_both = []
    for n in range(4):
        wait_all(coming[n])
        if n < 2:
            coming.append(fetch(n + 2))
        coming_both.append(fetch_both(TILES[n]))
        grad_act = lax.dot_general(rows[...], down[quarter[n], :], NT, preferred_element_type=F32)
        pre_gate = pre_gate_all[:, quarter[n]]
        sig = jax.nn.sigmoid(pre_gate)
        d_both[:, H + n * 256:H + (n + 1) * 256] = (grad_act * (pre_gate * sig)).astype(BF)
        d_both[:, quarter[n]] = (
            grad_act * pre_up_all[:, quarter[n]] * (sig * (1.0 + pre_gate * (1.0 - sig)))
        ).astype(BF)
    perm = perm_pack()
    sent = []
    for tile, coming in zip(TILES, coming_both):
        wait_all(coming)
        lanes = lanes_of(tile)
        rows[:, lanes] = lax.dot_general(d_both[...], both[lanes, :], NT, preferred_element_type=F32).astype(BF)
        if tile is not REST:
            pack(rows, out, perm, tile)
            sent.append(copies.start(out.at[:, lanes], out_hbm.at[:, lanes]))
    wait_all(sent)


def combine_kernel(
    msg_hbm, mix_hbm, spread_hbm, teacher_hbm, student_hbm, upstream_hbm, out_hbm,
    msg, rows, mix, spread, teacher, student, upstream, out, sems,
):
    copies = Copies(sems)
    arriving = [copies.start(msg_hbm.at[:, lanes_of(c)], msg.at[:, lanes_of(c)]) for c in CHUNKS]
    small = [
        copies.start(mix_hbm, mix), copies.start(spread_hbm, spread), copies.start(teacher_hbm, teacher),
    ]
    perm = perm_unpack()
    for chunk, copy in zip(CHUNKS, arriving):
        copy.wait()
        unpack(msg, rows, perm, chunk)
    wait_all(small)
    perm = perm_pack()
    sent = []
    for tile in TILES:
        lanes = lanes_of(tile)
        mixed = jnp.dot(mix[...], rows[:, lanes], preferred_element_type=F32).astype(BF)
        student[:, lanes] = mixed
        upstream[:, lanes] = (mixed.astype(F32) - teacher[:, lanes].astype(F32)).astype(BF)
        rows[:, lanes] = jnp.dot(spread[...], upstream[:, lanes], preferred_element_type=F32).astype(BF)
        if tile is not REST:
            pack(rows, out, perm, tile)
            sent.append(copies.start(out.at[:, lanes], out_hbm.at[:, lanes]))
        if tile is CHUNKS[1]:
            done = slice(0, 12 * LANE)
            sent.append(copies.start(student.at[:, done], student_hbm.at[:, done]))
            sent.append(copies.start(upstream.at[:, done], upstream_hbm.at[:, done]))
    left = slice(12 * LANE, D)
    sent.append(copies.start(student.at[:, left], student_hbm.at[:, left]))
    sent.append(copies.start(upstream.at[:, left], upstream_hbm.at[:, left]))
    wait_all(sent)


def score_kernel(msg_ref, upstream_ref, ids_ref, scores_ref, out_ref, rows):
    perm = perm_unpack()
    for chunk in CHUNKS:
        unpack(msg_ref, rows, perm, chunk)
    inner = lax.dot_general(rows[...], upstream_ref[...], NT, preferred_element_type=F32)
    hits, hit, before = slots_of(ids_ref[...])
    by_expert = jnp.zeros((E, T), F32)
    for s in range(CAP):
        here = (hit > 0.5) & (before == float(s))
        by_expert = by_expert + jnp.where(here, inner[s * E:(s + 1) * E], 0.0)
    grad_w = jnp.concatenate([jnp.sum(hits[k] * by_expert, axis=0, keepdims=True) for k in range(K)], axis=0)
    sigma, total = gates_of(scores_ref[...])
    inner_sum = jnp.sum(grad_w * sigma, axis=0, keepdims=True)
    out_ref[...] = 2.5 * sigma * (1.0 - sigma) * (grad_w / total - inner_sum / (total * total))


def gather_kernel(msg_hbm, sum_hbm, out_hbm, msg, rows, sums, out, sems):
    copies = Copies(sems)
    arriving = [copies.start(msg_hbm.at[:, lanes_of(c)], msg.at[:, lanes_of(c)]) for c in CHUNKS]
    small = copies.start(sum_hbm, sums)
    perm = perm_unpack()
    sent = []
    for chunk, copy in zip(CHUNKS, arriving):
        copy.wait()
        if chunk is CHUNKS[0]:
            small.wait()
        unpack(msg, rows, perm, chunk)
        tiles = (chunk, REST) if chunk is CHUNKS[-1] else (chunk,)
        for tile in tiles:
            lanes = lanes_of(tile)
            out[:, lanes] = jnp.dot(sums[...], rows[:, lanes], preferred_element_type=F32).astype(BF)
            sent.append(copies.start(out.at[:, lanes], out_hbm.at[:, lanes]))
    wait_all(sent)


def struct(shape, dtype):
    return jax.ShapeDtypeStruct(shape, dtype)


PARAMS = pltpu.CompilerParams(vmem_limit_bytes=VMEM_LIMIT)
ROWS_SCRATCH = pltpu.VMEM((ROWS, D), BF)
MSG = struct((MSG_ROWS, MSG_COLS), BF)


def cost(flops, moved):
    return pl.CostEstimate(flops=flops, bytes_accessed=moved, transcendentals=0)


def vmem(shape, dtype=BF):
    return pltpu.VMEM(shape, dtype)


def own(kernel, name, outs, scratch, copies, estimate):
    return pl.pallas_call(
        kernel, name=name, out_shape=outs,
        in_specs=[pl.BlockSpec(memory_space=pl.ANY)] * copies[1],
        out_specs=jax.tree.map(lambda _: pl.BlockSpec(memory_space=pl.ANY), outs),
        scratch_shapes=scratch + [pltpu.SemaphoreType.DMA((copies[0],))],
        compiler_params=PARAMS, cost_estimate=estimate,
    )


MSG_SCRATCH = pltpu.VMEM((MSG_ROWS, MSG_COLS), BF)


def dispatch(ids, scales, codes):
    return own(
        dispatch_kernel, "dispatch", MSG,
        [vmem((K, T), jnp.int32), vmem((LANE, T), F32), vmem((T, D)), vmem((T, D)), ROWS_SCRATCH, MSG_SCRATCH],
        (9, 3), cost(2 * 10**9, 6 * 10**6),
    )(ids, scales, codes)


def tables(ids, scores):
    return pl.pallas_call(
        table_kernel, name="tables",
        out_shape=(struct((ROWS, T), BF), struct((T, ROWS), BF), struct((T, ROWS), BF)),
        compiler_params=PARAMS, cost_estimate=cost(10**8, 5 * 10**5),
    )(ids, scores)


def forward(msg, gate, up, down):
    pre = struct((ROWS, H), F32)
    return own(
        forward_kernel, "expert_forward", (MSG, pre, pre),
        [
            MSG_SCRATCH, ROWS_SCRATCH, vmem((D, H)), vmem((D, H)), vmem((H, D)), vmem((ROWS, H)),
            vmem((ROWS, H), F32), vmem((ROWS, H), F32), MSG_SCRATCH,
        ],
        (26, 4), cost(15 * 10**9, 37 * 10**6),
    )(msg, gate, up, down)


def backward(msg, pre_gate, pre_up, gate, up, down):
    return own(
        backward_kernel, "expert_backward", MSG,
        [
            MSG_SCRATCH, ROWS_SCRATCH, vmem((D, 2 * H)), vmem((H, D)), vmem((ROWS, H), F32), vmem((ROWS, H), F32),
            vmem((ROWS, 2 * H)), MSG_SCRATCH,
        ],
        (26, 6), cost(15 * 10**9, 37 * 10**6),
    )(msg, pre_gate, pre_up, gate, up, down)


def combine(msg, mix, spread, teacher):
    tok = struct((T, D), BF)
    return own(
        combine_kernel, "combine", (tok, tok, MSG),
        [
            MSG_SCRATCH, ROWS_SCRATCH, vmem((T, ROWS)), vmem((ROWS, T)), vmem((T, D)), vmem((T, D)), vmem((T, D)),
            MSG_SCRATCH,
        ],
        (13, 4), cost(3 * 10**9, 12 * 10**6),
    )(msg, mix, spread, teacher)


def scores_grad(msg, upstream, ids, scores):
    return pl.pallas_call(
        score_kernel, name="scores_grad",
        out_shape=struct((K, T), F32),
        scratch_shapes=[ROWS_SCRATCH],
        compiler_params=PARAMS, cost_estimate=cost(2 * 10**9, 6 * 10**6),
    )(msg, upstream, ids, scores)


def gather(msg, sums):
    return own(
        gather_kernel, "gather_tokens", struct((T, D), BF),
        [MSG_SCRATCH, ROWS_SCRATCH, vmem((T, ROWS)), vmem((T, D))],
        (8, 2), cost(2 * 10**9, 6 * 10**6),
    )(msg, sums)


def exchange(msg):
    return lax.all_to_all(msg, ("group", "local"), split_axis=0, concat_axis=0, tiled=True)


def per_device(token_codes, block_scales, route_scores, expert_ids, w_gate, w_up, w_down, teacher):
    ids = expert_ids.T
    scores = route_scores.T
    gate, up, down = w_gate[0], w_up[0], w_down[0]
    arrived = exchange(dispatch(ids, block_scales.T, token_codes))
    spread, mix, sums = tables(ids, scores)
    out_msg, pre_gate, pre_up = forward(arrived, gate, up, down)
    returned = exchange(out_msg)
    student_out, upstream, grad_msg = combine(returned, mix, spread, teacher)
    grad_in = exchange(grad_msg)
    grad_scores = scores_grad(returned, upstream, ids, scores)
    grad_back = exchange(backward(grad_in, pre_gate, pre_up, gate, up, down))
    grad_tokens = gather(grad_back, sums)
    return student_out, grad_tokens, grad_scores.T


def solution(mesh):
    rows = P(("group", "local"), None)
    mats = P(("group", "local"), None, None)
    return jax.shard_map(
        per_device, mesh=mesh, in_specs=(rows, rows, rows, rows, mats, mats, mats, rows),
        out_specs=(rows, rows, rows), check_vma=False,
    )
```

time: 340 us -> 343 us (level); the launches traced: 340 us -> 339 us
  no operation moved by 1% of the time
where the time goes in v2:
time: 343 us; the launch traced here: 339 us
  blocking collectives  134 us (39%)
  waiting for transfers between devices  110 us (32%)
  Pallas kernels  82.9 us (24%)
  starting transfers between devices  11.2 us (3%)
    all_to_all x2, blocking collectives, exchange(): lax.all_to_all(msg, ('group', 'local'), split_axis=0, concat_axis=0, tile...  134 us
    all_to_all x2, waiting for transfers between devices, exchange(): lax.all_to_all(msg, ('group', 'local'), split_axis=0, concat_axis=0, tile...  110 us
    pallas_call x1, Pallas kernels, backward(): own(backward_kernel, 'expert_backward', MSG, [MSG_SCRATCH, ROWS_SCRATCH,...  30.2 us
    pallas_call x1, Pallas kernels, forward(): own(forward_kernel, 'expert_forward', (MSG, pre, pre), [MSG_SCRATCH, ROWS...  24.2 us
    all_to_all x2, starting transfers between devices, exchange(): lax.all_to_all(msg, ('group', 'local'), split_axis=0, concat_axis=0, tile...  11.2 us
    pallas_call x1, Pallas kernels, combine(): own(combine_kernel, 'combine', (tok, tok, MSG), [MSG_SCRATCH, ROWS_SCRATC...  8.61 us
  transfers between devices with their start and end apart: 2, of which 2 were waited for; matrix products, arithmetic and copies ran while one was open for 0% of the time, Pallas kernels for 2%

profile of v2, /device:TPU:1, one launch (start us, length us, event | category | flops | bytes accessed | tf_op | source)
XLA Modules:
  0.0 338.6 jit_solution(8603934891510233942)
XLA Ops:
  0.6 6.3 %dispatch.1 = bf16[1024,2304]{1,0:T(8,128)(2,1)} custom-call(s32[4,128]{1,0:T(4,128)} %bitcast.28, f32[28,128]{1,0:T(8,128)} %bitcast.27, bf16[128,3584]{1,0:T(8,128)(2,1)} %codes_hbm.1), custom_call_target="tpu_custom_call" | custom-call | flops 2000000000 | bytes 6000000 | tf_op jit(solution)/shard_map/dispatch/pallas_call | solution.py:375
  7.0 70.1 %all_to_all.44 = bf16[128,8,2304]{2,1,0:T(8,128)(2,1)} all-to-all(bf16[128,8,2304]{2,1,0:T(8,128)(2,1)} %bitcast.20), channel_id=1, replica_groups=mesh['group'=4,'local'=32] {'group','local'}, dimensions={0} | all-to-all | bytes 9437184 | tf_op jit(solution)/shard_map/all_to_all | solution.py:443
  77.0 24.2 %expert_forward.1 = (bf16[1024,2304]{1,0:T(8,128)(2,1)}, f32[640,1024]{1,0:T(8,128)}, f32[640,1024]{1,0:T(8,128)}) custom-call(bf16[1024,2304]{1,0:T(8,128)(2,1)} %bitcast.18, bf16[3584,1024]{1,0:T(8,128)(2,1)} %bitcast.21, bf16[3584,1024]{1,0:T(8,128)(2,1)} %bitcast.23, bf16[1024,3584]{1,0:T(8,128)(2,1)} %bitcast.25), custom_call_target="tpu_custom_call" | custom-call | flops 15000000512 | bytes 37000000 | tf_op jit(solution)/shard_map/expert_forward/pallas_call | solution.py:392
  101.3 5.6 %all-to-all-start.1 = ((bf16[128,8,2304]{2,1,0:T(8,128)(2,1)}), bf16[128,8,2304]{2,1,0:T(8,128)(2,1)}, u32[]{:S(2)}, u32[]{:S(2)}) async-start(bf16[128,8,2304]{2,1,0:T(8,128)(2,1)} %bitcast.15), calls=%async_computation.1 | async-start | bytes 9437184 | tf_op jit(solution)/shard_map/all_to_all | solution.py:443
  106.9 1.8 tables.1
  108.7 56.9 %all-to-all-done.1 = bf16[128,8,2304]{2,1,0:T(8,128)(2,1)} async-done(((bf16[128,8,2304]{2,1,0:T(8,128)(2,1)}), bf16[128,8,2304]{2,1,0:T(8,128)(2,1)}, u32[]{:S(2)}, u32[]{:S(2)}) %all-to-all-start.1) | async-done | bytes 4718624 | tf_op jit(solution)/shard_map/all_to_all | solution.py:443
  165.5 8.6 %combine.1 = (bf16[128,3584]{1,0:T(8,128)(2,1)}, bf16[128,3584]{1,0:T(8,128)(2,1)}, bf16[1024,2304]{1,0:T(8,128)(2,1)}) custom-call(bf16[1024,2304]{1,0:T(8,128)(2,1)} %bitcast.8.msg_hbm.msg_ref, bf16[128,640]{1,0:T(8,128)(2,1)} %get-tuple-element.13.mix_hbm, bf16[640,128]{1,0:T(8,128)(2,1)} %get-tuple-element.14.spread_hbm, bf16[128,3584]{1,0:T(8,128)(2,1)} %teacher_hbm.1), custom_call_target="tpu_custom_call" | custom-call | flops 3000000000 | bytes 12000000 | tf_op jit(solution)/shard_map/combine/pallas_call | solution.py:415
  174.1 63.9 %all_to_all.45 = bf16[128,8,2304]{2,1,0:T(8,128)(2,1)} all-to-all(bf16[128,8,2304]{2,1,0:T(8,128)(2,1)} %bitcast.17), channel_id=1, replica_groups=mesh['group'=4,'local'=32] {'group','local'}, dimensions={0} | all-to-all | bytes 9437184 | tf_op jit(solution)/shard_map/all_to_all | solution.py:443
  238.0 30.2 %expert_backward.1 = bf16[1024,2304]{1,0:T(8,128)(2,1)} custom-call(bf16[1024,2304]{1,0:T(8,128)(2,1)} %bitcast.19, f32[640,1024]{1,0:T(8,128)} %get-tuple-element.17.pre_gate_hbm, f32[640,1024]{1,0:T(8,128)} %get-tuple-element.18.pre_up_hbm, bf16[3584,1024]{1,0:T(8,128)(2,1)} %bitcast.22, bf16[3584,1024]{1,0:T(8,128)(2,1)} %bitcast.24, ...), custom_call_target="tpu_custom_call" | custom-call | flops 15000000512 | bytes 37000000 | tf_op jit(solution)/shard_map/expert_backward/pallas_call | solution.py:403
  268.2 5.6 %all-to-all-start.3 = ((bf16[128,8,2304]{2,1,0:T(8,128)(2,1)}), bf16[128,8,2304]{2,1,0:T(8,128)(2,1)}, u32[]{:S(2)}, u32[]{:S(2)}) async-start(bf16[128,8,2304]{2,1,0:T(8,128)(2,1)} %bitcast.16), calls=%async_computation.3 | async-start | bytes 9437184 | tf_op jit(solution)/shard_map/all_to_all | solution.py:443
  273.8 5.9 %scores_grad.1 = f32[4,128]{1,0:T(4,128)} custom-call(bf16[1024,2304]{1,0:T(8,128)(2,1)} %bitcast.8.msg_hbm.msg_ref, bf16[128,3584]{1,0:T(8,128)(2,1)} %get-tuple-element.20.upstream_ref, s32[4,128]{1,0:T(4,128)} %bitcast.30, f32[4,128]{1,0:T(4,128)} %bitcast.32), custom_call_target="tpu_custom_call" | custom-call | flops 2000000000 | bytes 6000000 | tf_op jit(solution)/shard_map/scores_grad/pallas_call | solution.py:426
  279.7 52.8 %all-to-all-done.3 = bf16[128,8,2304]{2,1,0:T(8,128)(2,1)} async-done(((bf16[128,8,2304]{2,1,0:T(8,128)(2,1)}), bf16[128,8,2304]{2,1,0:T(8,128)(2,1)}, u32[]{:S(2)}, u32[]{:S(2)}) %all-to-all-start.3) | async-done | bytes 4718624 | tf_op jit(solution)/shard_map/all_to_all | solution.py:443
  332.4 5.9 %gather_tokens.1 = bf16[128,3584]{1,0:T(8,128)(2,1)} custom-call(bf16[1024,2304]{1,0:T(8,128)(2,1)} %bitcast.13.msg_hbm, bf16[128,640]{1,0:T(8,128)(2,1)} %get-tuple-element.19.sum_hbm), custom_call_target="tpu_custom_call" | custom-call | flops 2000000000 | bytes 6000000 | tf_op jit(solution)/shard_map/gather_tokens/pallas_call | solution.py:435
Async XLA Ops:
  101.3 64.2 %all-to-all-start.1 = ((bf16[128,8,2304]{2,1,0:T(8,128)(2,1)}), bf16[128,8,2304]{2,1,0:T(8,128)(2,1)}, u32[]{:S(2)}, u32[]{:S(2)}) async-start(bf16[128,8,2304]{2,1,0:T(8,128)(2,1)} %bitcast.15), calls=%async_computation.1 | async-start | bytes 9437184 | tf_op jit(solution)/shard_map/all_to_all | solution.py:443
  268.2 64.2 %all-to-all-start.3 = ((bf16[128,8,2304]{2,1,0:T(8,128)(2,1)}), bf16[128,8,2304]{2,1,0:T(8,128)(2,1)}, u32[]{:S(2)}, u32[]{:S(2)}) async-start(bf16[128,8,2304]{2,1,0:T(8,128)(2,1)} %bitcast.16), calls=%async_computation.3 | async-start | bytes 9437184 | tf_op jit(solution)/shard_map/all_to_all | solution.py:443

commit v3 on v2

v3 whole, which is shorter than its diff:
```python
import jax
import jax.numpy as jnp
from jax import lax
from jax.experimental import pallas as pl
from jax.experimental.pallas import tpu as pltpu
from jax.sharding import PartitionSpec as P

T = 128
E = 128
D = 3584
H = 1024
K = 4
CAP = 5
LANE = 128
NB = D // LANE
MAIN = 18
TAIL = NB - MAIN
ROWS = CAP * E
MSG_ROWS = 8 * E
MSG_COLS = MAIN * LANE
GP = 32
GR = GP * 8
F32 = jnp.float32
BF = jnp.bfloat16
NT = (((1,), (1,)), ((), ()))
CHUNKS = ((0, 6), (6, 6), (12, 6))
REST = (MAIN, TAIL)
TILES = (REST,) + CHUNKS


def lanes_of(chunk):
    return slice(chunk[0] * LANE, (chunk[0] + chunk[1]) * LANE)


def cell_of(slot, block):
    index = slot * TAIL + block
    return 5 + index // MAIN, index % MAIN


CELLS = {cell_of(s, b): (s, b) for s in range(CAP) for b in range(TAIL)}


def iota(shape, dim):
    return lax.broadcasted_iota(jnp.int32, shape, dim)


def one_hot(cond):
    return jnp.where(cond, 1.0, 0.0).astype(BF)


def perm_unpack():
    r = iota((GR, GR), 0)
    return one_hot(iota((GR, GR), 1) == (r % GP) * 8 + r // GP)


def perm_pack():
    r = iota((GR, GR), 0)
    return one_hot(iota((GR, GR), 1) == (r % 8) * GP + r // 8)


def unpack(msg_ref, rows_ref, perm, chunk):
    first, count = chunk
    lanes = lanes_of(chunk)
    for g in range(E // GP):
        moved = jnp.dot(perm, msg_ref[g * GR:(g + 1) * GR, lanes], preferred_element_type=F32).astype(BF)
        for s in range(CAP):
            rows_ref[s * E + g * GP:s * E + (g + 1) * GP, lanes] = moved[s * GP:(s + 1) * GP]
        for q in range(5, 8):
            for c in range(first, first + count):
                if (q, c) in CELLS:
                    s, b = CELLS[q, c]
                    rows_ref[s * E + g * GP:s * E + (g + 1) * GP, lanes_of((MAIN + b, 1))] = (
                        moved[q * GP:(q + 1) * GP, lanes_of((c - first, 1))]
                    )


def pack(rows_ref, msg_ref, perm, chunk):
    first, count = chunk
    lanes = lanes_of(chunk)
    blank = jnp.zeros((GP, LANE), BF)
    for g in range(E // GP):
        parts = [rows_ref[s * E + g * GP:s * E + (g + 1) * GP, lanes] for s in range(CAP)]
        for q in range(5, 8):
            cells = []
            for c in range(first, first + count):
                if (q, c) in CELLS:
                    s, b = CELLS[q, c]
                    cells.append(rows_ref[s * E + g * GP:s * E + (g + 1) * GP, lanes_of((MAIN + b, 1))])
                else:
                    cells.append(blank)
            parts.append(jnp.concatenate(cells, axis=1))
        stacked = jnp.concatenate(parts, axis=0)
        msg_ref[g * GR:(g + 1) * GR, lanes] = jnp.dot(perm, stacked, preferred_element_type=F32).astype(BF)


class Copies:
    def __init__(self, sems):
        self.sems = sems
        self.used = 0

    def start(self, source, target):
        copy = pltpu.make_async_copy(source, target, self.sems.at[self.used])
        self.used += 1
        copy.start()
        return copy


def wait_all(copies):
    for copy in copies:
        copy.wait()


def slots_of(ids):
    expert = iota((E, T), 0)
    hits = [jnp.where(ids[k:k + 1, :] == expert, 1.0, 0.0) for k in range(K)]
    hit = hits[0] + hits[1] + hits[2] + hits[3]
    earlier = one_hot(iota((T, T), 0) < iota((T, T), 1))
    before = jnp.dot(hit.astype(BF), earlier, preferred_element_type=F32)
    return hits, hit, before


def gates_of(scores):
    sigma = jax.nn.sigmoid(scores)
    total = jnp.sum(sigma, axis=0, keepdims=True)
    return sigma, total


def dispatch_kernel(
    ids_hbm, scores_hbm, scales_hbm, codes_hbm, msg_ref, spread_ref, mix_ref, sum_ref,
    ids, scores, scales, codes, rows, sems,
):
    copies = Copies(sems)
    ids_copy = copies.start(ids_hbm, ids)
    scales_copy = copies.start(scales_hbm, scales.at[0:NB, :])
    scores_copy = copies.start(scores_hbm, scores)
    code_copies = [copies.start(codes_hbm.at[:, lanes_of(t)], codes.at[:, lanes_of(t)]) for t in TILES]
    perm = perm_pack()
    ids_copy.wait()
    hits, hit, before = slots_of(ids[...])
    here = [(hit > 0.5) & (before == float(s)) for s in range(CAP)]
    pick = jnp.concatenate([one_hot(h) for h in here], axis=0)
    scales_copy.wait()
    scale = scales[...].T
    for tile, copy in zip(TILES, code_copies):
        copy.wait()
        for j in range(tile[0], tile[0] + tile[1]):
            lanes = lanes_of((j, 1))
            codes[:, lanes] = (codes[:, lanes].astype(F32) * scale[:, j:j + 1]).astype(BF)
        lanes = lanes_of(tile)
        rows[:, lanes] = jnp.dot(pick, codes[:, lanes], preferred_element_type=F32).astype(BF)
        if tile is not REST:
            pack(rows, msg_ref, perm, tile)
    scores_copy.wait()
    sigma, total = gates_of(scores[...])
    weight = (2.5 * sigma / total).astype(BF).astype(F32)
    weighted = hits[0] * weight[0:1]
    for k in range(1, K):
        weighted = weighted + hits[k] * weight[k:k + 1]
    for s in range(CAP):
        part = slice(s * E, (s + 1) * E)
        spread = jnp.where(here[s], weighted, 0.0)
        spread_ref[part, :] = spread.astype(BF)
        mix_ref[:, part] = spread.T.astype(BF)
        sum_ref[:, part] = jnp.where(here[s], 1.0, 0.0).T.astype(BF)


def forward_kernel(msg_ref, gate_ref, up_ref, down_ref, out_ref, silu_ref, slope_ref, rows, active):
    perm = perm_unpack()
    for chunk in CHUNKS:
        unpack(msg_ref, rows, perm, chunk)
    for n in range(0, H, 256):
        lanes = slice(n, n + 256)
        pre_gate = jnp.dot(rows[...], gate_ref[:, lanes], preferred_element_type=F32)
        pre_up = jnp.dot(rows[...], up_ref[:, lanes], preferred_element_type=F32)
        sig = jax.nn.sigmoid(pre_gate)
        silu = pre_gate * sig
        active[:, lanes] = (silu * pre_up).astype(BF)
        silu_ref[:, lanes] = silu.astype(BF)
        slope_ref[:, lanes] = (pre_up * (sig * (1.0 + pre_gate * (1.0 - sig)))).astype(BF)
    perm = perm_pack()
    for tile in TILES:
        lanes = lanes_of(tile)
        rows[:, lanes] = jnp.dot(active[...], down_ref[:, lanes], preferred_element_type=F32).astype(BF)
        if tile is not REST:
            pack(rows, out_ref, perm, tile)


def backward_kernel(msg_ref, silu_ref, slope_ref, gate_ref, up_ref, down_ref, out_ref, rows, d_gate, d_up):
    perm = perm_unpack()
    for chunk in CHUNKS:
        unpack(msg_ref, rows, perm, chunk)
    for n in range(0, H, 256):
        lanes = slice(n, n + 256)
        grad_act = lax.dot_general(rows[...], down_ref[lanes, :], NT, preferred_element_type=F32)
        d_up[:, lanes] = (grad_act * silu_ref[:, lanes].astype(F32)).astype(BF)
        d_gate[:, lanes] = (grad_act * slope_ref[:, lanes].astype(F32)).astype(BF)
    perm = perm_pack()
    for tile in TILES:
        lanes = lanes_of(tile)
        summed = lax.dot_general(d_gate[...], gate_ref[lanes, :], NT, preferred_element_type=F32)
        summed = summed + lax.dot_general(d_up[...], up_ref[lanes, :], NT, preferred_element_type=F32)
        rows[:, lanes] = summed.astype(BF)
        if tile is not REST:
            pack(rows, out_ref, perm, tile)


def combine_kernel(
    msg_ref, mix_ref, spread_ref, teacher_ref, ids_ref, scores_ref, student_hbm, grad_scores_ref, out_ref,
    rows, student, inner, sems,
):
    copies = Copies(sems)
    perm = perm_unpack()
    for chunk in CHUNKS:
        unpack(msg_ref, rows, perm, chunk)
    perm = perm_pack()
    sent = []
    for tile in TILES:
        lanes = lanes_of(tile)
        mixed = jnp.dot(mix_ref[...], rows[:, lanes], preferred_element_type=F32).astype(BF)
        student[:, lanes] = mixed
        sent.append(copies.start(student.at[:, lanes], student_hbm.at[:, lanes]))
        upstream = (mixed.astype(F32) - teacher_ref[:, lanes].astype(F32)).astype(BF)
        grad_out = jnp.dot(spread_ref[...], upstream, preferred_element_type=F32)
        product = grad_out * rows[:, lanes].astype(F32)
        partial = product[:, 0:LANE]
        for j in range(1, tile[1]):
            partial = partial + product[:, lanes_of((j, 1))]
        inner[...] = partial if tile is REST else inner[...] + partial
        rows[:, lanes] = grad_out.astype(BF)
        if tile is not REST:
            pack(rows, out_ref, perm, tile)
    slot_inner = jnp.sum(inner[...], axis=1, keepdims=True)
    hits, hit, before = slots_of(ids_ref[...])
    by_expert = jnp.zeros((E, T), F32)
    for s in range(CAP):
        here = (hit > 0.5) & (before == float(s))
        by_expert = by_expert + jnp.where(here, slot_inner[s * E:(s + 1) * E], 0.0)
    sigma, total = gates_of(scores_ref[...])
    weight = (2.5 * sigma / total).astype(BF).astype(F32)
    weighted_inner = jnp.concatenate(
        [jnp.sum(hits[k] * by_expert, axis=0, keepdims=True) for k in range(K)], axis=0
    )
    grad_w = weighted_inner / weight
    inner_sum = jnp.sum(grad_w * sigma, axis=0, keepdims=True)
    grad_scores_ref[...] = 2.5 * sigma * (1.0 - sigma) * (grad_w / total - inner_sum / (total * total))
    wait_all(sent)


def gather_kernel(msg_ref, sum_ref, out_hbm, rows, out, sems):
    copies = Copies(sems)
    perm = perm_unpack()
    sent = []
    for chunk in CHUNKS:
        unpack(msg_ref, rows, perm, chunk)
        tiles = (REST, chunk) if chunk is CHUNKS[-1] else (chunk,)
        for tile in tiles:
            lanes = lanes_of(tile)
            out[:, lanes] = jnp.dot(sum_ref[...], rows[:, lanes], preferred_element_type=F32).astype(BF)
            sent.append(copies.start(out.at[:, lanes], out_hbm.at[:, lanes]))
    wait_all(sent)


def struct(shape, dtype=BF):
    return jax.ShapeDtypeStruct(shape, dtype)


def vmem(shape, dtype=BF):
    return pltpu.VMEM(shape, dtype)


MSG = struct((MSG_ROWS, MSG_COLS))
ROWS_SCRATCH = vmem((ROWS, D))
ON_CHIP = pl.BlockSpec(memory_space=pltpu.VMEM)
IN_HBM = pl.BlockSpec(memory_space=pltpu.HBM)


def on_chip(array):
    return pltpu.with_memory_space_constraint(array, pltpu.VMEM)


def in_hbm(array):
    return pltpu.with_memory_space_constraint(array, pltpu.HBM)


def own(kernel, name, outs, scratch, limit, estimate, in_specs, out_specs):
    return pl.pallas_call(
        kernel, name=name, out_shape=outs, in_specs=in_specs, out_specs=out_specs, scratch_shapes=scratch,
        compiler_params=pltpu.CompilerParams(vmem_limit_bytes=limit * 2**20),
        cost_estimate=pl.CostEstimate(flops=estimate[0], bytes_accessed=estimate[1], transcendentals=0),
    )


def copy_sems(count):
    return pltpu.SemaphoreType.DMA((count,))


HID = struct((ROWS, H))
TOK_HBM = pltpu.HBM((T, D), BF)


def dispatch(ids, scores, scales, codes):
    return own(
        dispatch_kernel, "dispatch", (MSG, struct((ROWS, T)), struct((T, ROWS)), struct((T, ROWS))),
        [vmem((K, T), jnp.int32), vmem((K, T), F32), vmem((LANE, T), F32), vmem((T, D)), ROWS_SCRATCH, copy_sems(7)],
        16, (60 * 10**9, 6 * 10**6), [IN_HBM] * 4, (ON_CHIP,) * 4,
    )(in_hbm(ids), in_hbm(scores), in_hbm(scales), in_hbm(codes))


def forward(msg, gate, up, down):
    return own(
        forward_kernel, "expert_forward", (MSG, HID, HID), [ROWS_SCRATCH, vmem((ROWS, H))],
        14, (15 * 10**9, 10**7), [ON_CHIP] * 4, (ON_CHIP,) * 3,
    )(on_chip(msg), on_chip(gate), on_chip(up), on_chip(down))


def backward(msg, silu, slope, gate, up, down):
    return own(
        backward_kernel, "expert_backward", MSG, [ROWS_SCRATCH, vmem((ROWS, H)), vmem((ROWS, H))],
        14, (15 * 10**9, 3 * 10**7), [ON_CHIP] * 6, ON_CHIP,
    )(on_chip(msg), on_chip(silu), on_chip(slope), on_chip(gate), on_chip(up), on_chip(down))


def combine(msg, mix, spread, teacher, ids, scores):
    return own(
        combine_kernel, "combine", (TOK_HBM, struct((K, T), F32), MSG),
        [ROWS_SCRATCH, vmem((T, D)), vmem((ROWS, LANE), F32), copy_sems(4)],
        14, (60 * 10**9, 10**7), [ON_CHIP] * 6, (IN_HBM, ON_CHIP, ON_CHIP),
    )(on_chip(msg), on_chip(mix), on_chip(spread), on_chip(teacher), on_chip(ids), on_chip(scores))


def gather(msg, sums):
    return own(
        gather_kernel, "gather_tokens", TOK_HBM, [ROWS_SCRATCH, vmem((T, D)), copy_sems(4)],
        12, (2 * 10**9, 6 * 10**6), [ON_CHIP] * 2, IN_HBM,
    )(on_chip(msg), on_chip(sums))


def exchange(msg):
    return lax.all_to_all(msg, ("group", "local"), split_axis=0, concat_axis=0, tiled=True)


def per_device(token_codes, block_scales, route_scores, expert_ids, w_gate, w_up, w_down, teacher):
    ids = expert_ids.T
    scores = route_scores.T
    gate, up, down = w_gate[0], w_up[0], w_down[0]
    msg, spread, mix, sums = dispatch(ids, scores, block_scales.T, token_codes)
    out_msg, silu, slope = forward(exchange(msg), gate, up, down)
    student_out, grad_scores, grad_msg = combine(exchange(out_msg), mix, spread, teacher, ids, scores)
    grad_back = backward(exchange(grad_msg), silu, slope, gate, up, down)
    grad_tokens = gather(exchange(grad_back), sums)
    return student_out, grad_tokens, grad_scores.T


def solution(mesh):
    rows = P(("group", "local"), None)
    mats = P(("group", "local"), None, None)
    return jax.shard_map(
        per_device, mesh=mesh, in_specs=(rows, rows, rows, rows, mats, mats, mats, rows),
        out_specs=(rows, rows, rows), check_vma=False,
    )
```

time: 343 us -> 319 us (0.930)
  blocking collectives: 134 us -> 260 us
  waiting for transfers between devices: 110 us -> 0 us
  Pallas kernels: 82.9 us -> 51.5 us
  starting transfers between devices: 11.2 us -> 0 us
    all_to_all x2 -> x4, blocking collectives: 134 us -> 260 us  [exchange(): lax.all_to_all(msg, ('group', 'local'), split_axis=0, concat_axis=0, tile...]
    all_to_all x2 -> x0, waiting for transfers between devices: 110 us -> none  [exchange(): lax.all_to_all(msg, ('group', 'local'), split_axis=0, concat_axis=0, tile...]
    pallas_call x7 -> x5, Pallas kernels: 82.9 us -> 51.5 us  [the longest x1 19.2 us: backward(): own(backward_kernel, 'expert_backward', MSG, [ROWS_SCRATCH, vmem((ROWS, H...]
    all_to_all x2 -> x0, starting transfers between devices: 11.2 us -> none  [exchange(): lax.all_to_all(msg, ('group', 'local'), split_axis=0, concat_axis=0, tile...]
  transfers between devices with their start and end apart: 2 -> 0, of which waited for: 2 -> 0; matrix products, arithmetic and copies ran while one was open for 0% -> 0% of each run, Pallas kernels for 2% -> 0%
where the time goes in v3:
time: 319 us; the launch traced here: 315 us
  blocking collectives  260 us (82%)
  Pallas kernels  51.5 us (16%)
    all_to_all x4, blocking collectives, exchange(): lax.all_to_all(msg, ('group', 'local'), split_axis=0, concat_axis=0, tile...  260 us
    pallas_call x1, Pallas kernels, backward(): own(backward_kernel, 'expert_backward', MSG, [ROWS_SCRATCH, vmem((ROWS, H...  19.2 us
    pallas_call x1, Pallas kernels, forward(): own(forward_kernel, 'expert_forward', (MSG, HID, HID), [ROWS_SCRATCH, vme...  17.9 us

profile of v3, /device:TPU:1, one launch (start us, length us, event | category | flops | bytes accessed | tf_op | source)
XLA Modules:
  0.0 315.3 jit_solution(17037942923333457635)
XLA Ops:
  0.6 0.0 copy-start.1
  0.6 0.0 copy-start.3
  0.7 5.5 %dispatch.1 = (bf16[1024,2304]{1,0:T(8,128)(2,1)S(1)}, bf16[640,128]{1,0:T(8,128)(2,1)S(1)}, bf16[128,640]{1,0:T(8,128)(2,1)S(1)}, bf16[128,640]{1,0:T(8,128)(2,1)S(1)}) custom-call(s32[4,128]{1,0:T(4,128)} %bitcast.29, f32[4,128]{1,0:T(4,128)} %bitcast.31, f32[28,128]{1,0:T(8,128)} %bitcast.33, bf16[128,3584]{1,0:T(8,128)(2,1)} %codes_hbm.1), custom_call_target="tpu_custom_call" | custom-call | flops 60000002048 | bytes 6000000 | tf_op jit(solution)/shard_map/dispatch/pallas_call | solution.py:302
  6.2 0.0 copy-start
  6.2 69.8 %all_to_all.44 = bf16[128,8,2304]{2,1,0:T(8,128)(2,1)S(1)} all-to-all(bf16[128,8,2304]{2,1,0:T(8,128)(2,1)S(1)} %bitcast.17), channel_id=1, replica_groups=mesh['group'=4,'local'=32] {'group','local'}, dimensions={0} | all-to-all | bytes 9437184 | tf_op jit(solution)/shard_map/all_to_all | solution.py:339
  75.9 0.0 copy-done.1
  75.9 0.0 copy-done.3
  75.9 0.0 copy-done
  75.9 17.9 %expert_forward.1 = (bf16[1024,2304]{1,0:T(8,128)(2,1)S(1)}, bf16[640,1024]{1,0:T(8,128)(2,1)S(1)}, bf16[640,1024]{1,0:T(8,128)(2,1)S(1)}) custom-call(bf16[1024,2304]{1,0:T(8,128)(2,1)S(1)} %bitcast.18, bf16[3584,1024]{1,0:T(8,128)(2,1)S(1)} %bitcast.23, bf16[3584,1024]{1,0:T(8,128)(2,1)S(1)} %bitcast.25, bf16[1024,3584]{1,0:T(8,128)(2,1)S(1)} %bitcast.27), custom_call_target="tpu_custom_call" | custom-call | flops 15000000512 | bytes 10000000 | tf_op jit(solution)/shard_map/expert_forward/pallas_call | solution.py:310
  93.8 0.0 copy-start.4
  93.8 0.0 copy-start.5
  93.8 0.0 copy-start.6
  93.8 63.3 %all_to_all.45 = bf16[128,8,2304]{2,1,0:T(8,128)(2,1)S(1)} all-to-all(bf16[128,8,2304]{2,1,0:T(8,128)(2,1)S(1)} %bitcast.19), channel_id=1, replica_groups=mesh['group'=4,'local'=32] {'group','local'}, dimensions={0} | all-to-all | bytes 9437184 | tf_op jit(solution)/shard_map/all_to_all | solution.py:339
  157.2 0.0 copy-done.4
  157.2 0.0 copy-done.5
  157.2 0.0 copy-done.6
  157.2 5.9 %combine.1 = (bf16[128,3584]{1,0:T(8,128)(2,1)}, f32[4,128]{1,0:T(4,128)}, bf16[1024,2304]{1,0:T(8,128)(2,1)S(1)}) custom-call(bf16[1024,2304]{1,0:T(8,128)(2,1)S(1)} %bitcast.15, bf16[128,640]{1,0:T(8,128)(2,1)S(1)} %get-tuple-element.15.mix_ref, bf16[640,128]{1,0:T(8,128)(2,1)S(1)} %get-tuple-element.16.spread_ref, bf16[128,3584]{1,0:T(8,128)(2,1)S(1)} %copy-done.4, ...), custom_call_target="tpu_custom_call" | custom-call | flops 60000002048 | bytes 10000000 | tf_op jit(solution)/shard_map/combine/pallas_call | solution.py:324
  163.1 63.3 %all_to_all.46 = bf16[128,8,2304]{2,1,0:T(8,128)(2,1)S(1)} all-to-all(bf16[128,8,2304]{2,1,0:T(8,128)(2,1)S(1)} %bitcast.16), channel_id=1, replica_groups=mesh['group'=4,'local'=32] {'group','local'}, dimensions={0} | all-to-all | bytes 9437184 | tf_op jit(solution)/shard_map/all_to_all | solution.py:339
  226.4 0.0 copy-start.2
  226.4 3.1 copy-done.2
  229.5 19.2 %expert_backward.1 = bf16[1024,2304]{1,0:T(8,128)(2,1)S(1)} custom-call(bf16[1024,2304]{1,0:T(8,128)(2,1)S(1)} %bitcast.20, bf16[640,1024]{1,0:T(8,128)(2,1)S(1)} %get-tuple-element.19.silu_ref, bf16[640,1024]{1,0:T(8,128)(2,1)S(1)} %get-tuple-element.20.slope_ref, bf16[3584,1024]{1,0:T(8,128)(2,1)S(1)} %bitcast.24, bf16[3584,1024]{1,0:T(8,128)(2,1)S(1)} %bitcast.26, ...), custom_call_target="tpu_custom_call" | custom-call | flops 15000000512 | bytes 30000000 | tf_op jit(solution)/shard_map/expert_backward/pallas_call | solution.py:317
  248.7 63.3 %all_to_all.47 = bf16[128,8,2304]{2,1,0:T(8,128)(2,1)S(1)} all-to-all(bf16[128,8,2304]{2,1,0:T(8,128)(2,1)S(1)} %bitcast.21), channel_id=1, replica_groups=mesh['group'=4,'local'=32] {'group','local'}, dimensions={0} | all-to-all | bytes 9437184 | tf_op jit(solution)/shard_map/all_to_all | solution.py:339
  312.0 3.0 gather_tokens.1
Async XLA Ops:
  0.6 75.3 %copy-start.1 = (bf16[1,3584,1024]{2,1,0:T(8,128)(2,1)S(1)}, bf16[1,3584,1024]{2,1,0:T(8,128)(2,1)}, u32[]{:S(2)}) copy-start(bf16[1,3584,1024]{2,1,0:T(8,128)(2,1)} %param.13) | copy-start | bytes 22020100
  0.6 75.3 %copy-start.3 = (bf16[1,1024,3584]{2,1,0:T(8,128)(2,1)S(1)}, bf16[1,1024,3584]{2,1,0:T(8,128)(2,1)}, u32[]{:S(2)}) copy-start(bf16[1,1024,3584]{2,1,0:T(8,128)(2,1)} %param.14) | copy-start | bytes 22020100
  6.2 69.8 %copy-start = (bf16[1,3584,1024]{2,1,0:T(8,128)(2,1)S(1)}, bf16[1,3584,1024]{2,1,0:T(8,128)(2,1)}, u32[]{:S(2)}) copy-start(bf16[1,3584,1024]{2,1,0:T(8,128)(2,1)} %param.12) | copy-start | bytes 22020100
  93.8 63.4 %copy-start.4 = (bf16[128,3584]{1,0:T(8,128)(2,1)S(1)}, bf16[128,3584]{1,0:T(8,128)(2,1)}, u32[]{:S(2)}) copy-start(bf16[128,3584]{1,0:T(8,128)(2,1)} %teacher_ref.1) | copy-start | bytes 2752516
  93.8 63.3 %copy-start.5 = (s32[128,4]{0,1:T(4,128)S(1)}, s32[128,4]{0,1:T(4,128)}, u32[]{:S(2)}) copy-start(s32[128,4]{0,1:T(4,128)} %param.11) | copy-start | bytes 6148
  93.8 63.3 %copy-start.6 = (f32[128,4]{0,1:T(4,128)S(1)}, f32[128,4]{0,1:T(4,128)}, u32[]{:S(2)}) copy-start(f32[128,4]{0,1:T(4,128)} %param.10) | copy-start | bytes 6148
  226.4 3.1 copy-start.2

commit v4 on v3

--- a/solution.py
+++ b/solution.py
@@ -302,21 +302,21 @@
     return own(
         dispatch_kernel, "dispatch", (MSG, struct((ROWS, T)), struct((T, ROWS)), struct((T, ROWS))),
         [vmem((K, T), jnp.int32), vmem((K, T), F32), vmem((LANE, T), F32), vmem((T, D)), ROWS_SCRATCH, copy_sems(7)],
-        16, (60 * 10**9, 6 * 10**6), [IN_HBM] * 4, (ON_CHIP,) * 4,
+        9, (60 * 10**9, 6 * 10**6), [IN_HBM] * 4, (ON_CHIP,) * 4,
     )(in_hbm(ids), in_hbm(scores), in_hbm(scales), in_hbm(codes))
 
 
 def forward(msg, gate, up, down):
     return own(
         forward_kernel, "expert_forward", (MSG, HID, HID), [ROWS_SCRATCH, vmem((ROWS, H))],
-        14, (15 * 10**9, 10**7), [ON_CHIP] * 4, (ON_CHIP,) * 3,
+        9, (15 * 10**9, 10**7), [ON_CHIP] * 4, (ON_CHIP,) * 3,
     )(on_chip(msg), on_chip(gate), on_chip(up), on_chip(down))
 
 
 def backward(msg, silu, slope, gate, up, down):
     return own(
         backward_kernel, "expert_backward", MSG, [ROWS_SCRATCH, vmem((ROWS, H)), vmem((ROWS, H))],
-        14, (15 * 10**9, 3 * 10**7), [ON_CHIP] * 6, ON_CHIP,
+        11, (15 * 10**9, 3 * 10**7), [ON_CHIP] * 6, ON_CHIP,
     )(on_chip(msg), on_chip(silu), on_chip(slope), on_chip(gate), on_chip(up), on_chip(down))
 
 
@@ -324,14 +324,14 @@
     return own(
         combine_kernel, "combine", (TOK_HBM, struct((K, T), F32), MSG),
         [ROWS_SCRATCH, vmem((T, D)), vmem((ROWS, LANE), F32), copy_sems(4)],
-        14, (60 * 10**9, 10**7), [ON_CHIP] * 6, (IN_HBM, ON_CHIP, ON_CHIP),
+        9, (60 * 10**9, 10**7), [ON_CHIP] * 6, (IN_HBM, ON_CHIP, ON_CHIP),
     )(on_chip(msg), on_chip(mix), on_chip(spread), on_chip(teacher), on_chip(ids), on_chip(scores))
 
 
 def gather(msg, sums):
     return own(
         gather_kernel, "gather_tokens", TOK_HBM, [ROWS_SCRATCH, vmem((T, D)), copy_sems(4)],
-        12, (2 * 10**9, 6 * 10**6), [ON_CHIP] * 2, IN_HBM,
+        8, (2 * 10**9, 6 * 10**6), [ON_CHIP] * 2, IN_HBM,
     )(on_chip(msg), on_chip(sums))
 
 

time: 319 us -> 316 us (level)
  no operation moved by 1% of the time
where the time goes in v4:
time: 316 us; the launch traced here: 312 us
  blocking collectives  260 us (82%)
  Pallas kernels  51.6 us (16%)
    all_to_all x4, blocking collectives, exchange(): lax.all_to_all(msg, ('group', 'local'), split_axis=0, concat_axis=0, tile...  260 us
    pallas_call x1, Pallas kernels, backward(): own(backward_kernel, 'expert_backward', MSG, [ROWS_SCRATCH, vmem((ROWS, H...  19.3 us
    pallas_call x1, Pallas kernels, forward(): own(forward_kernel, 'expert_forward', (MSG, HID, HID), [ROWS_SCRATCH, vme...  17.9 us

profile of v4, /device:TPU:1, one launch (start us, length us, event | category | flops | bytes accessed | tf_op | source)
XLA Modules:
  0.0 312.3 jit_solution(15241064804465334803)
XLA Ops:
  0.6 0.0 copy-start.1
  0.6 0.0 copy-start.2
  0.7 5.5 %dispatch.1 = (bf16[1024,2304]{1,0:T(8,128)(2,1)S(1)}, bf16[640,128]{1,0:T(8,128)(2,1)S(1)}, bf16[128,640]{1,0:T(8,128)(2,1)S(1)}, bf16[128,640]{1,0:T(8,128)(2,1)S(1)}) custom-call(s32[4,128]{1,0:T(4,128)} %bitcast.31, f32[4,128]{1,0:T(4,128)} %bitcast.33, f32[28,128]{1,0:T(8,128)} %bitcast.35, bf16[128,3584]{1,0:T(8,128)(2,1)} %codes_hbm.1), custom_call_target="tpu_custom_call" | custom-call | flops 60000002048 | bytes 6000000 | tf_op jit(solution)/shard_map/dispatch/pallas_call | solution.py:302
  6.2 0.0 copy-start
  6.2 69.8 %all_to_all.44 = bf16[128,8,2304]{2,1,0:T(8,128)(2,1)S(1)} all-to-all(bf16[128,8,2304]{2,1,0:T(8,128)(2,1)S(1)} %bitcast.17), channel_id=1, replica_groups=mesh['group'=4,'local'=32] {'group','local'}, dimensions={0} | all-to-all | bytes 9437184 | tf_op jit(solution)/shard_map/all_to_all | solution.py:339
  75.9 0.0 copy-done.1
  75.9 0.0 copy-done.2
  75.9 0.0 copy-done
  75.9 17.9 %expert_forward.1 = (bf16[1024,2304]{1,0:T(8,128)(2,1)S(1)}, bf16[640,1024]{1,0:T(8,128)(2,1)S(1)}, bf16[640,1024]{1,0:T(8,128)(2,1)S(1)}) custom-call(bf16[1024,2304]{1,0:T(8,128)(2,1)S(1)} %bitcast.18, bf16[3584,1024]{1,0:T(8,128)(2,1)S(1)} %bitcast.23, bf16[3584,1024]{1,0:T(8,128)(2,1)S(1)} %bitcast.25, bf16[1024,3584]{1,0:T(8,128)(2,1)S(1)} %bitcast.27), custom_call_target="tpu_custom_call" | custom-call | flops 15000000512 | bytes 10000000 | tf_op jit(solution)/shard_map/expert_forward/pallas_call | solution.py:310
  93.8 0.0 copy-start.3
  93.8 0.0 copy-start.4
  93.8 0.0 copy-start.5
  93.8 0.0 slice-start
  93.9 63.3 %all_to_all.45 = bf16[128,8,2304]{2,1,0:T(8,128)(2,1)S(1)} all-to-all(bf16[128,8,2304]{2,1,0:T(8,128)(2,1)S(1)} %bitcast.19), channel_id=1, replica_groups=mesh['group'=4,'local'=32] {'group','local'}, dimensions={0} | all-to-all | bytes 9437184 | tf_op jit(solution)/shard_map/all_to_all | solution.py:339
  157.2 0.0 copy-done.3
  157.2 0.0 copy-done.4
  157.2 0.0 copy-done.5
  157.2 0.0 slice-start.1
  157.2 5.9 %combine.1 = (bf16[128,3584]{1,0:T(8,128)(2,1)}, f32[4,128]{1,0:T(4,128)}, bf16[1024,2304]{1,0:T(8,128)(2,1)S(1)}) custom-call(bf16[1024,2304]{1,0:T(8,128)(2,1)S(1)} %bitcast.15, bf16[128,640]{1,0:T(8,128)(2,1)S(1)} %get-tuple-element.15.mix_ref, bf16[640,128]{1,0:T(8,128)(2,1)S(1)} %get-tuple-element.16.spread_ref, bf16[128,3584]{1,0:T(8,128)(2,1)S(1)} %copy-done.3, ...), custom_call_target="tpu_custom_call" | custom-call | flops 60000002048 | bytes 10000000 | tf_op jit(solution)/shard_map/combine/pallas_call | solution.py:324
  163.1 63.3 %all_to_all.46 = bf16[128,8,2304]{2,1,0:T(8,128)(2,1)S(1)} all-to-all(bf16[128,8,2304]{2,1,0:T(8,128)(2,1)S(1)} %bitcast.16), channel_id=1, replica_groups=mesh['group'=4,'local'=32] {'group','local'}, dimensions={0} | all-to-all | bytes 9437184 | tf_op jit(solution)/shard_map/all_to_all | solution.py:339
  226.4 0.0 slice-done
  226.4 0.0 slice-done.1
  226.4 19.3 %expert_backward.1 = bf16[1024,2304]{1,0:T(8,128)(2,1)S(1)} custom-call(bf16[1024,2304]{1,0:T(8,128)(2,1)S(1)} %bitcast.20, bf16[640,1024]{1,0:T(8,128)(2,1)S(1)} %get-tuple-element.19.silu_ref, bf16[640,1024]{1,0:T(8,128)(2,1)S(1)} %get-tuple-element.20.slope_ref, bf16[3584,1024]{1,0:T(8,128)(2,1)S(1)} %bitcast.24, bf16[3584,1024]{1,0:T(8,128)(2,1)S(1)} %bitcast.26, ...), custom_call_target="tpu_custom_call" | custom-call | flops 15000000512 | bytes 30000000 | tf_op jit(solution)/shard_map/expert_backward/pallas_call | solution.py:317
  245.7 63.3 %all_to_all.47 = bf16[128,8,2304]{2,1,0:T(8,128)(2,1)S(1)} all-to-all(bf16[128,8,2304]{2,1,0:T(8,128)(2,1)S(1)} %bitcast.21), channel_id=1, replica_groups=mesh['group'=4,'local'=32] {'group','local'}, dimensions={0} | all-to-all | bytes 9437184 | tf_op jit(solution)/shard_map/all_to_all | solution.py:339
  309.0 3.0 gather_tokens.1
  (1 shorter events, 0.0 us)
Async XLA Ops:
  0.6 75.3 %copy-start.1 = (bf16[1,3584,1024]{2,1,0:T(8,128)(2,1)S(1)}, bf16[1,3584,1024]{2,1,0:T(8,128)(2,1)}, u32[]{:S(2)}) copy-start(bf16[1,3584,1024]{2,1,0:T(8,128)(2,1)} %param.13) | copy-start | bytes 22020100
  0.6 75.3 %copy-start.2 = (bf16[1,1024,3584]{2,1,0:T(8,128)(2,1)S(1)}, bf16[1,1024,3584]{2,1,0:T(8,128)(2,1)}, u32[]{:S(2)}) copy-start(bf16[1,1024,3584]{2,1,0:T(8,128)(2,1)} %param.14) | copy-start | bytes 22020100
  6.2 69.8 %copy-start = (bf16[1,3584,1024]{2,1,0:T(8,128)(2,1)S(1)}, bf16[1,3584,1024]{2,1,0:T(8,128)(2,1)}, u32[]{:S(2)}) copy-start(bf16[1,3584,1024]{2,1,0:T(8,128)(2,1)} %param.12) | copy-start | bytes 22020100
  93.8 63.4 %copy-start.3 = (bf16[128,3584]{1,0:T(8,128)(2,1)S(1)}, bf16[128,3584]{1,0:T(8,128)(2,1)}, u32[]{:S(2)}) copy-start(bf16[128,3584]{1,0:T(8,128)(2,1)} %teacher_ref.1) | copy-start | bytes 2752516
  93.8 63.4 %copy-start.4 = (s32[128,4]{0,1:T(4,128)S(1)}, s32[128,4]{0,1:T(4,128)}, u32[]{:S(2)}) copy-start(s32[128,4]{0,1:T(4,128)} %param.11) | copy-start | bytes 6148
  93.8 63.4 %copy-start.5 = (f32[128,4]{0,1:T(4,128)S(1)}, f32[128,4]{0,1:T(4,128)}, u32[]{:S(2)}) copy-start(f32[128,4]{0,1:T(4,128)} %param.10) | copy-start | bytes 6148
  93.8 132.6 %slice-start = ((s8[7340032]{0:T(1024)(128)(4,1)}), s8[4194304]{0:T(1024)(128)(4,1)S(1)}, s32[]{:S(2)}) async-start(s8[7340032]{0:T(1024)(128)(4,1)} %bitcast.28), calls=%async_computation.4 | async-start | bytes 8388608
  157.2 69.2 %slice-start.1 = ((s8[7340032]{0:T(1024)(128)(4,1)}), s8[3145728]{0:T(1024)(128)(4,1)S(1)}, s32[]{:S(2)}) async-start(s8[7340032]{0:T(1024)(128)(4,1)} %bitcast.28), calls=%async_computation.5 | async-start | bytes 6291456

commit v5 on v4

--- a/solution.py
+++ b/solution.py
@@ -13,33 +13,23 @@
 CAP = 5
 LANE = 128
 NB = D // LANE
-MAIN = 18
-TAIL = NB - MAIN
 ROWS = CAP * E
-MSG_ROWS = 8 * E
-MSG_COLS = MAIN * LANE
-GP = 32
-GR = GP * 8
+LINES = CAP - 1
+QUART = NB // LINES
+MSG_COLS = (NB + QUART) * LANE
+GP = 64
+GR = GP * LINES
 F32 = jnp.float32
 BF = jnp.bfloat16
 NT = (((1,), (1,)), ((), ()))
-CHUNKS = ((0, 6), (6, 6), (12, 6))
-REST = (MAIN, TAIL)
-TILES = (REST,) + CHUNKS
+TILES = ((0, 10), (10, 10), (20, 8))
+LAST = (NB, QUART)
 
 
 def lanes_of(chunk):
     return slice(chunk[0] * LANE, (chunk[0] + chunk[1]) * LANE)
 
 
-def cell_of(slot, block):
-    index = slot * TAIL + block
-    return 5 + index // MAIN, index % MAIN
-
-
-CELLS = {cell_of(s, b): (s, b) for s in range(CAP) for b in range(TAIL)}
-
-
 def iota(shape, dim):
     return lax.broadcasted_iota(jnp.int32, shape, dim)
 
@@ -50,47 +40,47 @@
 
 def perm_unpack():
     r = iota((GR, GR), 0)
-    return one_hot(iota((GR, GR), 1) == (r % GP) * 8 + r // GP)
+    return one_hot(iota((GR, GR), 1) == (r % GP) * LINES + r // GP)
 
 
 def perm_pack():
     r = iota((GR, GR), 0)
-    return one_hot(iota((GR, GR), 1) == (r % 8) * GP + r // 8)
+    return one_hot(iota((GR, GR), 1) == (r % LINES) * GP + r // LINES)
+
+
+def slot_rows(slot, g):
+    return slice(slot * E + g * GP, slot * E + (g + 1) * GP)
 
 
 def unpack(msg_ref, rows_ref, perm, chunk):
-    first, count = chunk
+    lines = msg_ref.reshape(E * LINES, MSG_COLS)
     lanes = lanes_of(chunk)
     for g in range(E // GP):
-        moved = jnp.dot(perm, msg_ref[g * GR:(g + 1) * GR, lanes], preferred_element_type=F32).astype(BF)
-        for s in range(CAP):
-            rows_ref[s * E + g * GP:s * E + (g + 1) * GP, lanes] = moved[s * GP:(s + 1) * GP]
-        for q in range(5, 8):
-            for c in range(first, first + count):
-                if (q, c) in CELLS:
-                    s, b = CELLS[q, c]
-                    rows_ref[s * E + g * GP:s * E + (g + 1) * GP, lanes_of((MAIN + b, 1))] = (
-                        moved[q * GP:(q + 1) * GP, lanes_of((c - first, 1))]
-                    )
+        moved = jnp.dot(perm, lines[g * GR:(g + 1) * GR, lanes], preferred_element_type=F32).astype(BF)
+        for q in range(LINES):
+            line = moved[q * GP:(q + 1) * GP]
+            if chunk is LAST:
+                rows_ref[slot_rows(LINES, g), lanes_of((q * QUART, QUART))] = line
+            else:
+                rows_ref[slot_rows(q, g), lanes] = line
+
+
+def unpack_all(msg_ref, rows_ref):
+    perm = perm_unpack()
+    for chunk in (LAST,) + TILES:
+        unpack(msg_ref, rows_ref, perm, chunk)
 
 
 def pack(rows_ref, msg_ref, perm, chunk):
-    first, count = chunk
+    lines = msg_ref.reshape(E * LINES, MSG_COLS)
     lanes = lanes_of(chunk)
-    blank = jnp.zeros((GP, LANE), BF)
     for g in range(E // GP):
-        parts = [rows_ref[s * E + g * GP:s * E + (g + 1) * GP, lanes] for s in range(CAP)]
-        for q in range(5, 8):
-            cells = []
-            for c in range(first, first + count):
-                if (q, c) in CELLS:
-                    s, b = CELLS[q, c]
-                    cells.append(rows_ref[s * E + g * GP:s * E + (g + 1) * GP, lanes_of((MAIN + b, 1))])
-                else:
-                    cells.append(blank)
-            parts.append(jnp.concatenate(cells, axis=1))
+        if chunk is LAST:
+            parts = [rows_ref[slot_rows(LINES, g), lanes_of((q * QUART, QUART))] for q in range(LINES)]
+        else:
+            parts = [rows_ref[slot_rows(q, g), lanes] for q in range(LINES)]
         stacked = jnp.concatenate(parts, axis=0)
-        msg_ref[g * GR:(g + 1) * GR, lanes] = jnp.dot(perm, stacked, preferred_element_type=F32).astype(BF)
+        lines[g * GR:(g + 1) * GR, lanes] = jnp.dot(perm, stacked, preferred_element_type=F32).astype(BF)
 
 
 class Copies:
@@ -148,8 +138,8 @@
             codes[:, lanes] = (codes[:, lanes].astype(F32) * scale[:, j:j + 1]).astype(BF)
         lanes = lanes_of(tile)
         rows[:, lanes] = jnp.dot(pick, codes[:, lanes], preferred_element_type=F32).astype(BF)
-        if tile is not REST:
-            pack(rows, msg_ref, perm, tile)
+        pack(rows, msg_ref, perm, tile)
+    pack(rows, msg_ref, perm, LAST)
     scores_copy.wait()
     sigma, total = gates_of(scores[...])
     weight = (2.5 * sigma / total).astype(BF).astype(F32)
@@ -165,9 +155,7 @@
 
 
 def forward_kernel(msg_ref, gate_ref, up_ref, down_ref, out_ref, silu_ref, slope_ref, rows, active):
-    perm = perm_unpack()
-    for chunk in CHUNKS:
-        unpack(msg_ref, rows, perm, chunk)
+    unpack_all(msg_ref, rows)
     for n in range(0, H, 256):
         lanes = slice(n, n + 256)
         pre_gate = jnp.dot(rows[...], gate_ref[:, lanes], preferred_element_type=F32)
@@ -181,14 +169,12 @@
     for tile in TILES:
         lanes = lanes_of(tile)
         rows[:, lanes] = jnp.dot(active[...], down_ref[:, lanes], preferred_element_type=F32).astype(BF)
-        if tile is not REST:
-            pack(rows, out_ref, perm, tile)
+        pack(rows, out_ref, perm, tile)
+    pack(rows, out_ref, perm, LAST)
 
 
 def backward_kernel(msg_ref, silu_ref, slope_ref, gate_ref, up_ref, down_ref, out_ref, rows, d_gate, d_up):
-    perm = perm_unpack()
-    for chunk in CHUNKS:
-        unpack(msg_ref, rows, perm, chunk)
+    unpack_all(msg_ref, rows)
     for n in range(0, H, 256):
         lanes = slice(n, n + 256)
         grad_act = lax.dot_general(rows[...], down_ref[lanes, :], NT, preferred_element_type=F32)
@@ -200,8 +186,8 @@
         summed = lax.dot_general(d_gate[...], gate_ref[lanes, :], NT, preferred_element_type=F32)
         summed = summed + lax.dot_general(d_up[...], up_ref[lanes, :], NT, preferred_element_type=F32)
         rows[:, lanes] = summed.astype(BF)
-        if tile is not REST:
-            pack(rows, out_ref, perm, tile)
+        pack(rows, out_ref, perm, tile)
+    pack(rows, out_ref, perm, LAST)
 
 
 def combine_kernel(
@@ -209,9 +195,7 @@
     rows, student, inner, sems,
 ):
     copies = Copies(sems)
-    perm = perm_unpack()
-    for chunk in CHUNKS:
-        unpack(msg_ref, rows, perm, chunk)
+    unpack_all(msg_ref, rows)
     perm = perm_pack()
     sent = []
     for tile in TILES:
@@ -225,10 +209,10 @@
         partial = product[:, 0:LANE]
         for j in range(1, tile[1]):
             partial = partial + product[:, lanes_of((j, 1))]
-        inner[...] = partial if tile is REST else inner[...] + partial
+        inner[...] = partial if tile is TILES[0] else inner[...] + partial
         rows[:, lanes] = grad_out.astype(BF)
-        if tile is not REST:
-            pack(rows, out_ref, perm, tile)
+        pack(rows, out_ref, perm, tile)
+    pack(rows, out_ref, perm, LAST)
     slot_inner = jnp.sum(inner[...], axis=1, keepdims=True)
     hits, hit, before = slots_of(ids_ref[...])
     by_expert = jnp.zeros((E, T), F32)
@@ -250,13 +234,12 @@
     copies = Copies(sems)
     perm = perm_unpack()
     sent = []
-    for chunk in CHUNKS:
-        unpack(msg_ref, rows, perm, chunk)
-        tiles = (REST, chunk) if chunk is CHUNKS[-1] else (chunk,)
-        for tile in tiles:
-            lanes = lanes_of(tile)
-            out[:, lanes] = jnp.dot(sum_ref[...], rows[:, lanes], preferred_element_type=F32).astype(BF)
-            sent.append(copies.start(out.at[:, lanes], out_hbm.at[:, lanes]))
+    unpack(msg_ref, rows, perm, LAST)
+    for tile in TILES:
+        unpack(msg_ref, rows, perm, tile)
+        lanes = lanes_of(tile)
+        out[:, lanes] = jnp.dot(sum_ref[...], rows[:, lanes], preferred_element_type=F32).astype(BF)
+        sent.append(copies.start(out.at[:, lanes], out_hbm.at[:, lanes]))
     wait_all(sent)
 
 
@@ -268,7 +251,7 @@
     return pltpu.VMEM(shape, dtype)
 
 
-MSG = struct((MSG_ROWS, MSG_COLS))
+MSG = struct((E, LINES, MSG_COLS))
 ROWS_SCRATCH = vmem((ROWS, D))
 ON_CHIP = pl.BlockSpec(memory_space=pltpu.VMEM)
 IN_HBM = pl.BlockSpec(memory_space=pltpu.HBM)
@@ -301,7 +284,7 @@
 def dispatch(ids, scores, scales, codes):
     return own(
         dispatch_kernel, "dispatch", (MSG, struct((ROWS, T)), struct((T, ROWS)), struct((T, ROWS))),
-        [vmem((K, T), jnp.int32), vmem((K, T), F32), vmem((LANE, T), F32), vmem((T, D)), ROWS_SCRATCH, copy_sems(7)],
+        [vmem((K, T), jnp.int32), vmem((K, T), F32), vmem((LANE, T), F32), vmem((T, D)), ROWS_SCRATCH, copy_sems(6)],
         9, (60 * 10**9, 6 * 10**6), [IN_HBM] * 4, (ON_CHIP,) * 4,
     )(in_hbm(ids), in_hbm(scores), in_hbm(scales), in_hbm(codes))
 
@@ -323,14 +306,14 @@
 def combine(msg, mix, spread, teacher, ids, scores):
     return own(
         combine_kernel, "combine", (TOK_HBM, struct((K, T), F32), MSG),
-        [ROWS_SCRATCH, vmem((T, D)), vmem((ROWS, LANE), F32), copy_sems(4)],
+        [ROWS_SCRATCH, vmem((T, D)), vmem((ROWS, LANE), F32), copy_sems(3)],
         9, (60 * 10**9, 10**7), [ON_CHIP] * 6, (IN_HBM, ON_CHIP, ON_CHIP),
     )(on_chip(msg), on_chip(mix), on_chip(spread), on_chip(teacher), on_chip(ids), on_chip(scores))
 
 
 def gather(msg, sums):
     return own(
-        gather_kernel, "gather_tokens", TOK_HBM, [ROWS_SCRATCH, vmem((T, D)), copy_sems(4)],
+        gather_kernel, "gather_tokens", TOK_HBM, [ROWS_SCRATCH, vmem((T, D)), copy_sems(3)],
         8, (2 * 10**9, 6 * 10**6), [ON_CHIP] * 2, IN_HBM,
     )(on_chip(msg), on_chip(sums))
 

time: 316 us -> 309 us (0.978)
  blocking collectives: 260 us -> 255 us
    all_to_all x4, blocking collectives: 260 us -> 255 us  [exchange(): lax.all_to_all(msg, ('group', 'local'), split_axis=0, concat_axis=0, tile...]
where the time goes in v5:
time: 309 us; the launch traced here: 306 us
  blocking collectives  255 us (83%)
  Pallas kernels  49.7 us (16%)
    all_to_all x4, blocking collectives, exchange(): lax.all_to_all(msg, ('group', 'local'), split_axis=0, concat_axis=0, tile...  255 us
    pallas_call x1, Pallas kernels, backward(): own(backward_kernel, 'expert_backward', MSG, [ROWS_SCRATCH, vmem((ROWS, H...  18.9 us
    pallas_call x1, Pallas kernels, forward(): own(forward_kernel, 'expert_forward', (MSG, HID, HID), [ROWS_SCRATCH, vme...  17.6 us

profile of v5, /device:TPU:1, one launch (start us, length us, event | category | flops | bytes accessed | tf_op | source)
XLA Modules:
  0.0 305.6 jit_solution(12693235916145766475)
XLA Ops:
  0.6 0.0 copy-start.1
  0.6 0.0 copy-start.2
  0.7 4.9 %dispatch.1 = (bf16[128,4,4480]{2,1,0:T(4,128)(2,1)S(1)}, bf16[640,128]{1,0:T(8,128)(2,1)S(1)}, bf16[128,640]{1,0:T(8,128)(2,1)S(1)}, bf16[128,640]{1,0:T(8,128)(2,1)S(1)}) custom-call(s32[4,128]{1,0:T(4,128)} %bitcast.15, f32[4,128]{1,0:T(4,128)} %bitcast.17, f32[28,128]{1,0:T(8,128)} %bitcast.19, bf16[128,3584]{1,0:T(8,128)(2,1)} %codes_hbm.1), custom_call_target="tpu_custom_call" | custom-call | flops 60000002048 | bytes 6000000 | tf_op jit(solution)/shard_map/dispatch/pallas_call | solution.py:285
  5.5 0.0 copy-start
  5.5 68.4 %all_to_all.20.msg_ref = bf16[128,4,4480]{2,1,0:T(4,128)(2,1)S(1)} all-to-all(bf16[128,4,4480]{2,1,0:T(4,128)(2,1)S(1)} %get-tuple-element.13), channel_id=1, replica_groups=mesh['group'=4,'local'=32] {'group','local'}, dimensions={0} | all-to-all | bytes 9175040 | tf_op jit(solution)/shard_map/all_to_all | solution.py:322
  73.9 0.0 copy-done.1
  73.9 0.0 copy-done.2
  73.9 0.0 copy-done
  73.9 17.6 %expert_forward.1 = (bf16[128,4,4480]{2,1,0:T(4,128)(2,1)S(1)}, bf16[640,1024]{1,0:T(8,128)(2,1)S(1)}, bf16[640,1024]{1,0:T(8,128)(2,1)S(1)}) custom-call(bf16[128,4,4480]{2,1,0:T(4,128)(2,1)S(1)} %all_to_all.20.msg_ref, bf16[3584,1024]{1,0:T(8,128)(2,1)S(1)} %bitcast.7, bf16[3584,1024]{1,0:T(8,128)(2,1)S(1)} %bitcast.9, bf16[1024,3584]{1,0:T(8,128)(2,1)S(1)} %bitcast.11), custom_call_target="tpu_custom_call" | custom-call | flops 15000000512 | bytes 10000000 | tf_op jit(solution)/shard_map/expert_forward/pallas_call | solution.py:293
  91.5 0.0 copy-start.3
  91.5 0.0 copy-start.4
  91.6 0.0 copy-start.5
  91.6 0.0 slice-start
  91.6 62.2 %all_to_all.21.msg_ref = bf16[128,4,4480]{2,1,0:T(4,128)(2,1)S(1)} all-to-all(bf16[128,4,4480]{2,1,0:T(4,128)(2,1)S(1)} %get-tuple-element.14), channel_id=1, replica_groups=mesh['group'=4,'local'=32] {'group','local'}, dimensions={0} | all-to-all | bytes 9175040 | tf_op jit(solution)/shard_map/all_to_all | solution.py:322
  153.7 0.0 copy-done.3
  153.7 0.0 copy-done.4
  153.7 0.0 copy-done.5
  153.8 0.0 slice-start.1
  153.8 5.4 %combine.1 = (bf16[128,3584]{1,0:T(8,128)(2,1)}, f32[4,128]{1,0:T(4,128)}, bf16[128,4,4480]{2,1,0:T(4,128)(2,1)S(1)}) custom-call(bf16[128,4,4480]{2,1,0:T(4,128)(2,1)S(1)} %all_to_all.21.msg_ref, bf16[128,640]{1,0:T(8,128)(2,1)S(1)} %get-tuple-element.15.mix_ref, bf16[640,128]{1,0:T(8,128)(2,1)S(1)} %get-tuple-element.16.spread_ref, ...), custom_call_target="tpu_custom_call" | custom-call | flops 60000002048 | bytes 10000000 | tf_op jit(solution)/shard_map/combine/pallas_call | solution.py:307
  159.1 62.2 %all_to_all.22.msg_ref = bf16[128,4,4480]{2,1,0:T(4,128)(2,1)S(1)} all-to-all(bf16[128,4,4480]{2,1,0:T(4,128)(2,1)S(1)} %get-tuple-element.18), channel_id=1, replica_groups=mesh['group'=4,'local'=32] {'group','local'}, dimensions={0} | all-to-all | bytes 9175040 | tf_op jit(solution)/shard_map/all_to_all | solution.py:322
  221.3 0.0 slice-done
  221.3 0.0 slice-done.1
  221.3 18.9 %expert_backward.1 = bf16[128,4,4480]{2,1,0:T(4,128)(2,1)S(1)} custom-call(bf16[128,4,4480]{2,1,0:T(4,128)(2,1)S(1)} %all_to_all.22.msg_ref, bf16[640,1024]{1,0:T(8,128)(2,1)S(1)} %get-tuple-element.19.silu_ref, bf16[640,1024]{1,0:T(8,128)(2,1)S(1)} %get-tuple-element.20.slope_ref, bf16[3584,1024]{1,0:T(8,128)(2,1)S(1)} %bitcast.8, ...), custom_call_target="tpu_custom_call" | custom-call | flops 15000000512 | bytes 30000000 | tf_op jit(solution)/shard_map/expert_backward/pallas_call | solution.py:300
  240.2 62.2 %all_to_all.23.msg_ref = bf16[128,4,4480]{2,1,0:T(4,128)(2,1)S(1)} all-to-all(bf16[128,4,4480]{2,1,0:T(4,128)(2,1)S(1)} %expert_backward.1), channel_id=1, replica_groups=mesh['group'=4,'local'=32] {'group','local'}, dimensions={0} | all-to-all | bytes 9175040 | tf_op jit(solution)/shard_map/all_to_all | solution.py:322
  302.4 2.9 gather_tokens.1
  (1 shorter events, 0.0 us)
Async XLA Ops:
  0.6 73.3 %copy-start.1 = (bf16[1,3584,1024]{2,1,0:T(8,128)(2,1)S(1)}, bf16[1,3584,1024]{2,1,0:T(8,128)(2,1)}, u32[]{:S(2)}) copy-start(bf16[1,3584,1024]{2,1,0:T(8,128)(2,1)} %param.13) | copy-start | bytes 22020100
  0.6 73.3 %copy-start.2 = (bf16[1,1024,3584]{2,1,0:T(8,128)(2,1)S(1)}, bf16[1,1024,3584]{2,1,0:T(8,128)(2,1)}, u32[]{:S(2)}) copy-start(bf16[1,1024,3584]{2,1,0:T(8,128)(2,1)} %param.14) | copy-start | bytes 22020100
  5.5 68.4 %copy-start = (bf16[1,3584,1024]{2,1,0:T(8,128)(2,1)S(1)}, bf16[1,3584,1024]{2,1,0:T(8,128)(2,1)}, u32[]{:S(2)}) copy-start(bf16[1,3584,1024]{2,1,0:T(8,128)(2,1)} %param.12) | copy-start | bytes 22020100
  91.5 62.2 %copy-start.3 = (bf16[128,3584]{1,0:T(8,128)(2,1)S(1)}, bf16[128,3584]{1,0:T(8,128)(2,1)}, u32[]{:S(2)}) copy-start(bf16[128,3584]{1,0:T(8,128)(2,1)} %teacher_ref.1) | copy-start | bytes 2752516
  91.5 62.2 %copy-start.4 = (s32[128,4]{0,1:T(4,128)S(1)}, s32[128,4]{0,1:T(4,128)}, u32[]{:S(2)}) copy-start(s32[128,4]{0,1:T(4,128)} %param.11) | copy-start | bytes 6148
  91.6 62.2 %copy-start.5 = (f32[128,4]{0,1:T(4,128)S(1)}, f32[128,4]{0,1:T(4,128)}, u32[]{:S(2)}) copy-start(f32[128,4]{0,1:T(4,128)} %param.10) | copy-start | bytes 6148
  91.6 129.7 %slice-start = ((s8[7340032]{0:T(1024)(128)(4,1)}), s8[4194304]{0:T(1024)(128)(4,1)S(1)}, s32[]{:S(2)}) async-start(s8[7340032]{0:T(1024)(128)(4,1)} %bitcast.12), calls=%async_computation.4 | async-start | bytes 8388608
  153.8 67.6 %slice-start.1 = ((s8[7340032]{0:T(1024)(128)(4,1)}), s8[3145728]{0:T(1024)(128)(4,1)S(1)}, s32[]{:S(2)}) async-start(s8[7340032]{0:T(1024)(128)(4,1)} %bitcast.12), calls=%async_computation.5 | async-start | bytes 6291456

commit v6 on v5

v6 whole, which is shorter than its diff:
```python
import jax
import jax.numpy as jnp
from jax import lax
from jax.experimental import pallas as pl
from jax.experimental.pallas import tpu as pltpu
from jax.sharding import PartitionSpec as P

T = 128
E = 128
D = 3584
H = 1024
K = 4
CAP = 5
LANE = 128
NB = D // LANE
ROWS = CAP * E
LINES = CAP - 1
HEAD = E * LINES
QUART = NB // LINES
MSG_COLS = (NB + QUART) * LANE
GP = 64
GR = GP * LINES
F32 = jnp.float32
BF = jnp.bfloat16
NT = (((1,), (1,)), ((), ()))
TILES = ((0, 10), (10, 10), (20, 8))
LAST = (NB, QUART)


def lanes_of(chunk):
    return slice(chunk[0] * LANE, (chunk[0] + chunk[1]) * LANE)


def iota(shape, dim):
    return lax.broadcasted_iota(jnp.int32, shape, dim)


def one_hot(cond):
    return jnp.where(cond, 1.0, 0.0).astype(BF)


def perm_unpack():
    r = iota((GR, GR), 0)
    return one_hot(iota((GR, GR), 1) == (r % GP) * LINES + r // GP)


def perm_pack():
    r = iota((GR, GR), 0)
    return one_hot(iota((GR, GR), 1) == (r % LINES) * GP + r // LINES)


def lines_of(msg_ref):
    return msg_ref.reshape(HEAD, MSG_COLS)


def unpack_last(msg_ref, last_ref):
    perm = perm_unpack()
    lines = lines_of(msg_ref)
    for g in range(E // GP):
        moved = jnp.dot(perm, lines[g * GR:(g + 1) * GR, lanes_of(LAST)], preferred_element_type=F32).astype(BF)
        for q in range(LINES):
            last_ref[g * GP:(g + 1) * GP, lanes_of((q * QUART, QUART))] = moved[q * GP:(q + 1) * GP]


def unpack(msg_ref, rows_ref):
    unpack_last(msg_ref, rows_ref.at[HEAD:, :])
    lines = lines_of(msg_ref)
    for tile in TILES:
        rows_ref[:HEAD, lanes_of(tile)] = lines[:, lanes_of(tile)]


def put(msg_ref, last_ref, lanes, value):
    lines_of(msg_ref)[:, lanes] = value[:HEAD]
    last_ref[:, lanes] = value[HEAD:]


def pack_last(msg_ref, last_ref):
    perm = perm_pack()
    lines = lines_of(msg_ref)
    for g in range(E // GP):
        parts = [last_ref[g * GP:(g + 1) * GP, lanes_of((q * QUART, QUART))] for q in range(LINES)]
        stacked = jnp.concatenate(parts, axis=0)
        lines[g * GR:(g + 1) * GR, lanes_of(LAST)] = jnp.dot(perm, stacked, preferred_element_type=F32).astype(BF)


class Copies:
    def __init__(self, sems):
        self.sems = sems
        self.used = 0

    def start(self, source, target):
        copy = pltpu.make_async_copy(source, target, self.sems.at[self.used])
        self.used += 1
        copy.start()
        return copy


def wait_all(copies):
    for copy in copies:
        copy.wait()


def slots_of(ids):
    row = iota((ROWS, T), 0)
    expert = jnp.where(row < HEAD, row // LINES, row - HEAD)
    slot = jnp.where(row < HEAD, row % LINES, LINES)
    hits = [jnp.where(ids[k:k + 1, :] == expert, 1.0, 0.0) for k in range(K)]
    hit = hits[0] + hits[1] + hits[2] + hits[3]
    earlier = one_hot(iota((T, T), 0) < iota((T, T), 1))
    before = jnp.dot(hit.astype(BF), earlier, preferred_element_type=F32)
    return hits, (hit > 0.5) & (before == slot.astype(F32))


def gates_of(scores):
    sigma = jax.nn.sigmoid(scores)
    total = jnp.sum(sigma, axis=0, keepdims=True)
    return sigma, total


def dispatch_kernel(
    ids_hbm, scores_hbm, scales_hbm, codes_hbm, msg_ref, spread_ref, mix_ref, sum_ref,
    ids, scores, scales, codes, last, sems,
):
    copies = Copies(sems)
    ids_copy = copies.start(ids_hbm, ids)
    scales_copy = copies.start(scales_hbm, scales.at[0:NB, :])
    scores_copy = copies.start(scores_hbm, scores)
    code_copies = [copies.start(codes_hbm.at[:, lanes_of(t)], codes.at[:, lanes_of(t)]) for t in TILES]
    ids_copy.wait()
    hits, here = slots_of(ids[...])
    pick = one_hot(here)
    scales_copy.wait()
    scale = scales[...].T
    for tile, copy in zip(TILES, code_copies):
        copy.wait()
        for j in range(tile[0], tile[0] + tile[1]):
            lanes = lanes_of((j, 1))
            codes[:, lanes] = (codes[:, lanes].astype(F32) * scale[:, j:j + 1]).astype(BF)
        lanes = lanes_of(tile)
        put(msg_ref, last, lanes, jnp.dot(pick, codes[:, lanes], preferred_element_type=F32).astype(BF))
    pack_last(msg_ref, last)
    scores_copy.wait()
    sigma, total = gates_of(scores[...])
    weight = (2.5 * sigma / total).astype(BF).astype(F32)
    weighted = hits[0] * weight[0:1]
    for k in range(1, K):
        weighted = weighted + hits[k] * weight[k:k + 1]
    spread = jnp.where(here, weighted, 0.0)
    held = jnp.where(here, 1.0, 0.0)
    spread_ref[...] = spread.astype(BF)
    for n in range(0, ROWS, T):
        mix_ref[:, n:n + T] = spread[n:n + T].T.astype(BF)
        sum_ref[:, n:n + T] = held[n:n + T].T.astype(BF)


def forward_kernel(msg_ref, gate_ref, up_ref, down_ref, out_ref, silu_ref, slope_ref, rows, active):
    unpack(msg_ref, rows)
    for n in range(0, H, 256):
        lanes = slice(n, n + 256)
        pre_gate = jnp.dot(rows[...], gate_ref[:, lanes], preferred_element_type=F32)
        pre_up = jnp.dot(rows[...], up_ref[:, lanes], preferred_element_type=F32)
        sig = jax.nn.sigmoid(pre_gate)
        silu = pre_gate * sig
        active[:, lanes] = (silu * pre_up).astype(BF)
        silu_ref[:, lanes] = silu.astype(BF)
        slope_ref[:, lanes] = (pre_up * (sig * (1.0 + pre_gate * (1.0 - sig)))).astype(BF)
    last = rows.at[HEAD:, :]
    for tile in TILES:
        lanes = lanes_of(tile)
        put(out_ref, last, lanes, jnp.dot(active[...], down_ref[:, lanes], preferred_element_type=F32).astype(BF))
    pack_last(out_ref, last)


def backward_kernel(msg_ref, silu_ref, slope_ref, gate_ref, up_ref, down_ref, out_ref, rows, d_gate, d_up):
    unpack(msg_ref, rows)
    for n in range(0, H, 256):
        lanes = slice(n, n + 256)
        grad_act = lax.dot_general(rows[...], down_ref[lanes, :], NT, preferred_element_type=F32)
        d_up[:, lanes] = (grad_act * silu_ref[:, lanes].astype(F32)).astype(BF)
        d_gate[:, lanes] = (grad_act * slope_ref[:, lanes].astype(F32)).astype(BF)
    last = rows.at[HEAD:, :]
    for tile in TILES:
        lanes = lanes_of(tile)
        summed = lax.dot_general(d_gate[...], gate_ref[lanes, :], NT, preferred_element_type=F32)
        summed = summed + lax.dot_general(d_up[...], up_ref[lanes, :], NT, preferred_element_type=F32)
        put(out_ref, last, lanes, summed.astype(BF))
    pack_last(out_ref, last)


def summed_rows(table_ref, lines, last, lanes):
    head = jnp.dot(table_ref[:, :HEAD], lines[:, lanes], preferred_element_type=F32)
    return head + jnp.dot(table_ref[:, HEAD:], last[:, lanes], preferred_element_type=F32)


def combine_kernel(
    msg_ref, mix_ref, spread_ref, teacher_ref, ids_ref, scores_ref, student_hbm, grad_scores_ref, out_ref,
    last, sent_last, student, inner, sems,
):
    copies = Copies(sems)
    unpack_last(msg_ref, last)
    lines = lines_of(msg_ref)
    sent = []
    for tile in TILES:
        lanes = lanes_of(tile)
        mixed = summed_rows(mix_ref, lines, last, lanes).astype(BF)
        student[:, lanes] = mixed
        sent.append(copies.start(student.at[:, lanes], student_hbm.at[:, lanes]))
        upstream = (mixed.astype(F32) - teacher_ref[:, lanes].astype(F32)).astype(BF)
        grad_out = jnp.dot(spread_ref[...], upstream, preferred_element_type=F32)
        for part, held in ((slice(0, HEAD), lines), (slice(HEAD, ROWS), last)):
            product = grad_out[part] * held[:, lanes].astype(F32)
            partial = product[:, 0:LANE]
            for j in range(1, tile[1]):
                partial = partial + product[:, lanes_of((j, 1))]
            inner[part, :] = partial if tile is TILES[0] else inner[part, :] + partial
        put(out_ref, sent_last, lanes, grad_out.astype(BF))
    pack_last(out_ref, sent_last)
    hits, here = slots_of(ids_ref[...])
    slot_inner = jnp.where(here, jnp.sum(inner[...], axis=1, keepdims=True), 0.0)
    sigma, total = gates_of(scores_ref[...])
    weight = (2.5 * sigma / total).astype(BF).astype(F32)
    weighted_inner = jnp.concatenate(
        [jnp.sum(hits[k] * slot_inner, axis=0, keepdims=True) for k in range(K)], axis=0
    )
    grad_w = weighted_inner / weight
    inner_sum = jnp.sum(grad_w * sigma, axis=0, keepdims=True)
    grad_scores_ref[...] = 2.5 * sigma * (1.0 - sigma) * (grad_w / total - inner_sum / (total * total))
    wait_all(sent)


def gather_kernel(msg_ref, sum_ref, out_hbm, last, out, sems):
    copies = Copies(sems)
    unpack_last(msg_ref, last)
    lines = lines_of(msg_ref)
    sent = []
    for tile in TILES:
        lanes = lanes_of(tile)
        out[:, lanes] = summed_rows(sum_ref, lines, last, lanes).astype(BF)
        sent.append(copies.start(out.at[:, lanes], out_hbm.at[:, lanes]))
    wait_all(sent)


def struct(shape, dtype=BF):
    return jax.ShapeDtypeStruct(shape, dtype)


def vmem(shape, dtype=BF):
    return pltpu.VMEM(shape, dtype)


MSG = struct((E, LINES, MSG_COLS))
ROWS_SCRATCH = vmem((ROWS, D))
LAST_SCRATCH = vmem((E, D))
ON_CHIP = pl.BlockSpec(memory_space=pltpu.VMEM)
IN_HBM = pl.BlockSpec(memory_space=pltpu.HBM)


def on_chip(array):
    return pltpu.with_memory_space_constraint(array, pltpu.VMEM)


def in_hbm(array):
    return pltpu.with_memory_space_constraint(array, pltpu.HBM)


def own(kernel, name, outs, scratch, limit, estimate, in_specs, out_specs):
    return pl.pallas_call(
        kernel, name=name, out_shape=outs, in_specs=in_specs, out_specs=out_specs, scratch_shapes=scratch,
        compiler_params=pltpu.CompilerParams(vmem_limit_bytes=limit * 2**20),
        cost_estimate=pl.CostEstimate(flops=estimate[0], bytes_accessed=estimate[1], transcendentals=0),
    )


def copy_sems(count):
    return pltpu.SemaphoreType.DMA((count,))


HID = struct((ROWS, H))
TOK_HBM = pltpu.HBM((T, D), BF)


def dispatch(ids, scores, scales, codes):
    return own(
        dispatch_kernel, "dispatch", (MSG, struct((ROWS, T)), struct((T, ROWS)), struct((T, ROWS))),
        [vmem((K, T), jnp.int32), vmem((K, T), F32), vmem((LANE, T), F32), vmem((T, D)), LAST_SCRATCH, copy_sems(6)],
        9, (60 * 10**9, 6 * 10**6), [IN_HBM] * 4, (ON_CHIP,) * 4,
    )(in_hbm(ids), in_hbm(scores), in_hbm(scales), in_hbm(codes))


def forward(msg, gate, up, down):
    return own(
        forward_kernel, "expert_forward", (MSG, HID, HID), [ROWS_SCRATCH, vmem((ROWS, H))],
        9, (15 * 10**9, 10**7), [ON_CHIP] * 4, (ON_CHIP,) * 3,
    )(on_chip(msg), on_chip(gate), on_chip(up), on_chip(down))


def backward(msg, silu, slope, gate, up, down):
    return own(
        backward_kernel, "expert_backward", MSG, [ROWS_SCRATCH, vmem((ROWS, H)), vmem((ROWS, H))],
        11, (15 * 10**9, 3 * 10**7), [ON_CHIP] * 6, ON_CHIP,
    )(on_chip(msg), on_chip(silu), on_chip(slope), on_chip(gate), on_chip(up), on_chip(down))


def combine(msg, mix, spread, teacher, ids, scores):
    return own(
        combine_kernel, "combine", (TOK_HBM, struct((K, T), F32), MSG),
        [LAST_SCRATCH, LAST_SCRATCH, vmem((T, D)), vmem((ROWS, LANE), F32), copy_sems(3)],
        9, (60 * 10**9, 10**7), [ON_CHIP] * 6, (IN_HBM, ON_CHIP, ON_CHIP),
    )(on_chip(msg), on_chip(mix), on_chip(spread), on_chip(teacher), on_chip(ids), on_chip(scores))


def gather(msg, sums):
    return own(
        gather_kernel, "gather_tokens", TOK_HBM, [LAST_SCRATCH, vmem((T, D)), copy_sems(3)],
        8, (2 * 10**9, 6 * 10**6), [ON_CHIP] * 2, IN_HBM,
    )(on_chip(msg), on_chip(sums))


def exchange(msg):
    return lax.all_to_all(msg, ("group", "local"), split_axis=0, concat_axis=0, tiled=True)


def per_device(token_codes, block_scales, route_scores, expert_ids, w_gate, w_up, w_down, teacher):
    ids = expert_ids.T
    scores = route_scores.T
    gate, up, down = w_gate[0], w_up[0], w_down[0]
    msg, spread, mix, sums = dispatch(ids, scores, block_scales.T, token_codes)
    out_msg, silu, slope = forward(exchange(msg), gate, up, down)
    student_out, grad_scores, grad_msg = combine(exchange(out_msg), mix, spread, teacher, ids, scores)
    grad_back = backward(exchange(grad_msg), silu, slope, gate, up, down)
    grad_tokens = gather(exchange(grad_back), sums)
    return student_out, grad_tokens, grad_scores.T


def solution(mesh):
    rows = P(("group", "local"), None)
    mats = P(("group", "local"), None, None)
    return jax.shard_map(
        per_device, mesh=mesh, in_specs=(rows, rows, rows, rows, mats, mats, mats, rows),
        out_specs=(rows, rows, rows), check_vma=False,
    )
```

time: 309 us -> 297 us (0.961); the launches traced: 306 us -> 297 us
  Pallas kernels: 49.7 us -> 41.3 us
    pallas_call x1, Pallas kernels: 18.9 us -> 15.2 us  [backward(): own(backward_kernel, 'expert_backward', MSG, [ROWS_SCRATCH, vmem((ROWS, H...]
where the time goes in v6:
time: 297 us
  blocking collectives  255 us (86%)
  Pallas kernels  41.3 us (14%)
    all_to_all x4, blocking collectives, exchange(): lax.all_to_all(msg, ('group', 'local'), split_axis=0, concat_axis=0, tile...  255 us
    pallas_call x1, Pallas kernels, forward(): own(forward_kernel, 'expert_forward', (MSG, HID, HID), [ROWS_SCRATCH, vme...  15.2 us
    pallas_call x1, Pallas kernels, backward(): own(backward_kernel, 'expert_backward', MSG, [ROWS_SCRATCH, vmem((ROWS, H...  15.2 us

profile of v6, /device:TPU:1, one launch (start us, length us, event | category | flops | bytes accessed | tf_op | source)
XLA Modules:
  0.0 297.1 jit_solution(5047816560163359045)
XLA Ops:
  0.6 0.0 copy-start.1
  0.6 0.0 copy-start.2
  0.7 4.1 %dispatch.1 = (bf16[128,4,4480]{2,1,0:T(4,128)(2,1)S(1)}, bf16[640,128]{1,0:T(8,128)(2,1)S(1)}, bf16[128,640]{1,0:T(8,128)(2,1)S(1)}, bf16[128,640]{1,0:T(8,128)(2,1)S(1)}) custom-call(s32[4,128]{1,0:T(4,128)} %bitcast.15, f32[4,128]{1,0:T(4,128)} %bitcast.17, f32[28,128]{1,0:T(8,128)} %bitcast.19, bf16[128,3584]{1,0:T(8,128)(2,1)} %codes_hbm.1), custom_call_target="tpu_custom_call" | custom-call | flops 60000002048 | bytes 6000000 | tf_op jit(solution)/shard_map/dispatch/pallas_call | solution.py:283
  4.8 0.0 copy-start
  4.8 68.4 %all_to_all.20.msg_ref = bf16[128,4,4480]{2,1,0:T(4,128)(2,1)S(1)} all-to-all(bf16[128,4,4480]{2,1,0:T(4,128)(2,1)S(1)} %get-tuple-element.13), channel_id=1, replica_groups=mesh['group'=4,'local'=32] {'group','local'}, dimensions={0} | all-to-all | bytes 9175040 | tf_op jit(solution)/shard_map/all_to_all | solution.py:320
  73.2 0.0 copy-done.1
  73.2 0.0 copy-done.2
  73.2 0.0 copy-done
  73.2 15.2 %expert_forward.1 = (bf16[128,4,4480]{2,1,0:T(4,128)(2,1)S(1)}, bf16[640,1024]{1,0:T(8,128)(2,1)S(1)}, bf16[640,1024]{1,0:T(8,128)(2,1)S(1)}) custom-call(bf16[128,4,4480]{2,1,0:T(4,128)(2,1)S(1)} %all_to_all.20.msg_ref, bf16[3584,1024]{1,0:T(8,128)(2,1)S(1)} %bitcast.7, bf16[3584,1024]{1,0:T(8,128)(2,1)S(1)} %bitcast.9, bf16[1024,3584]{1,0:T(8,128)(2,1)S(1)} %bitcast.11), custom_call_target="tpu_custom_call" | custom-call | flops 15000000512 | bytes 10000000 | tf_op jit(solution)/shard_map/expert_forward/pallas_call | solution.py:291
  88.4 0.0 copy-start.3
  88.4 0.0 copy-start.4
  88.4 0.0 copy-start.5
  88.4 0.0 slice-start
  88.4 62.2 %all_to_all.21.msg_ref = bf16[128,4,4480]{2,1,0:T(4,128)(2,1)S(1)} all-to-all(bf16[128,4,4480]{2,1,0:T(4,128)(2,1)S(1)} %get-tuple-element.14), channel_id=1, replica_groups=mesh['group'=4,'local'=32] {'group','local'}, dimensions={0} | all-to-all | bytes 9175040 | tf_op jit(solution)/shard_map/all_to_all | solution.py:320
  150.6 0.0 copy-done.3
  150.6 0.0 copy-done.4
  150.6 0.0 copy-done.5
  150.6 0.0 slice-start.1
  150.6 4.6 %combine.1 = (bf16[128,3584]{1,0:T(8,128)(2,1)}, f32[4,128]{1,0:T(4,128)}, bf16[128,4,4480]{2,1,0:T(4,128)(2,1)S(1)}) custom-call(bf16[128,4,4480]{2,1,0:T(4,128)(2,1)S(1)} %all_to_all.21.msg_ref, bf16[128,640]{1,0:T(8,128)(2,1)S(1)} %get-tuple-element.15.mix_ref, bf16[640,128]{1,0:T(8,128)(2,1)S(1)} %get-tuple-element.16.spread_ref, ...), custom_call_target="tpu_custom_call" | custom-call | flops 60000002048 | bytes 10000000 | tf_op jit(solution)/shard_map/combine/pallas_call | solution.py:305
  155.3 62.2 %all_to_all.22.msg_ref = bf16[128,4,4480]{2,1,0:T(4,128)(2,1)S(1)} all-to-all(bf16[128,4,4480]{2,1,0:T(4,128)(2,1)S(1)} %get-tuple-element.18), channel_id=1, replica_groups=mesh['group'=4,'local'=32] {'group','local'}, dimensions={0} | all-to-all | bytes 9175040 | tf_op jit(solution)/shard_map/all_to_all | solution.py:320
  217.4 0.0 slice-done
  217.4 0.0 slice-done.1
  217.4 15.2 %expert_backward.1 = bf16[128,4,4480]{2,1,0:T(4,128)(2,1)S(1)} custom-call(bf16[128,4,4480]{2,1,0:T(4,128)(2,1)S(1)} %all_to_all.22.msg_ref, bf16[640,1024]{1,0:T(8,128)(2,1)S(1)} %get-tuple-element.19.silu_ref, bf16[640,1024]{1,0:T(8,128)(2,1)S(1)} %get-tuple-element.20.slope_ref, bf16[3584,1024]{1,0:T(8,128)(2,1)S(1)} %bitcast.8, ...), custom_call_target="tpu_custom_call" | custom-call | flops 15000000512 | bytes 30000000 | tf_op jit(solution)/shard_map/expert_backward/pallas_call | solution.py:298
  232.6 62.2 %all_to_all.23.msg_ref = bf16[128,4,4480]{2,1,0:T(4,128)(2,1)S(1)} all-to-all(bf16[128,4,4480]{2,1,0:T(4,128)(2,1)S(1)} %expert_backward.1), channel_id=1, replica_groups=mesh['group'=4,'local'=32] {'group','local'}, dimensions={0} | all-to-all | bytes 9175040 | tf_op jit(solution)/shard_map/all_to_all | solution.py:320
  294.8 2.1 gather_tokens.1
  (1 shorter events, 0.0 us)
Async XLA Ops:
  0.6 72.6 %copy-start.1 = (bf16[1,3584,1024]{2,1,0:T(8,128)(2,1)S(1)}, bf16[1,3584,1024]{2,1,0:T(8,128)(2,1)}, u32[]{:S(2)}) copy-start(bf16[1,3584,1024]{2,1,0:T(8,128)(2,1)} %param.13) | copy-start | bytes 22020100
  0.6 72.6 %copy-start.2 = (bf16[1,1024,3584]{2,1,0:T(8,128)(2,1)S(1)}, bf16[1,1024,3584]{2,1,0:T(8,128)(2,1)}, u32[]{:S(2)}) copy-start(bf16[1,1024,3584]{2,1,0:T(8,128)(2,1)} %param.14) | copy-start | bytes 22020100
  4.8 68.4 %copy-start = (bf16[1,3584,1024]{2,1,0:T(8,128)(2,1)S(1)}, bf16[1,3584,1024]{2,1,0:T(8,128)(2,1)}, u32[]{:S(2)}) copy-start(bf16[1,3584,1024]{2,1,0:T(8,128)(2,1)} %param.12) | copy-start | bytes 22020100
  88.4 62.2 %copy-start.3 = (bf16[128,3584]{1,0:T(8,128)(2,1)S(1)}, bf16[128,3584]{1,0:T(8,128)(2,1)}, u32[]{:S(2)}) copy-start(bf16[128,3584]{1,0:T(8,128)(2,1)} %teacher_ref.1) | copy-start | bytes 2752516
  88.4 62.2 %copy-start.4 = (s32[128,4]{0,1:T(4,128)S(1)}, s32[128,4]{0,1:T(4,128)}, u32[]{:S(2)}) copy-start(s32[128,4]{0,1:T(4,128)} %param.11) | copy-start | bytes 6148
  88.4 62.2 %copy-start.5 = (f32[128,4]{0,1:T(4,128)S(1)}, f32[128,4]{0,1:T(4,128)}, u32[]{:S(2)}) copy-start(f32[128,4]{0,1:T(4,128)} %param.10) | copy-start | bytes 6148
  88.4 129.0 %slice-start = ((s8[7340032]{0:T(1024)(128)(4,1)}), s8[4194304]{0:T(1024)(128)(4,1)S(1)}, s32[]{:S(2)}) async-start(s8[7340032]{0:T(1024)(128)(4,1)} %bitcast.12), calls=%async_computation.4 | async-start | bytes 8388608
  150.6 66.8 %slice-start.1 = ((s8[7340032]{0:T(1024)(128)(4,1)}), s8[3145728]{0:T(1024)(128)(4,1)S(1)}, s32[]{:S(2)}) async-start(s8[7340032]{0:T(1024)(128)(4,1)} %bitcast.12), calls=%async_computation.5 | async-start | bytes 6291456

commit v7 on v6

--- a/solution.py
+++ b/solution.py
@@ -118,7 +118,7 @@
 
 
 def dispatch_kernel(
-    ids_hbm, scores_hbm, scales_hbm, codes_hbm, msg_ref, spread_ref, mix_ref, sum_ref,
+    ids_hbm, scores_hbm, scales_hbm, codes_hbm, msg_ref, spread_ref, mix_ref,
     ids, scores, scales, codes, last, sems,
 ):
     copies = Copies(sems)
@@ -146,11 +146,22 @@
     for k in range(1, K):
         weighted = weighted + hits[k] * weight[k:k + 1]
     spread = jnp.where(here, weighted, 0.0)
-    held = jnp.where(here, 1.0, 0.0)
     spread_ref[...] = spread.astype(BF)
     for n in range(0, ROWS, T):
         mix_ref[:, n:n + T] = spread[n:n + T].T.astype(BF)
-        sum_ref[:, n:n + T] = held[n:n + T].T.astype(BF)
+
+
+def write_score_grad(inner, ids, scores, grad_scores_ref):
+    hits, here = slots_of(ids)
+    slot_inner = jnp.where(here, jnp.sum(inner, axis=1, keepdims=True), 0.0)
+    sigma, total = gates_of(scores)
+    weight = (2.5 * sigma / total).astype(BF).astype(F32)
+    weighted_inner = jnp.concatenate(
+        [jnp.sum(hits[k] * slot_inner, axis=0, keepdims=True) for k in range(K)], axis=0
+    )
+    grad_w = weighted_inner / weight
+    inner_sum = jnp.sum(grad_w * sigma, axis=0, keepdims=True)
+    grad_scores_ref[...] = 2.5 * sigma * (1.0 - sigma) * (grad_w / total - inner_sum / (total * total))
 
 
 def forward_kernel(msg_ref, gate_ref, up_ref, down_ref, out_ref, silu_ref, slope_ref, rows, active):
@@ -171,7 +182,11 @@
     pack_last(out_ref, last)
 
 
-def backward_kernel(msg_ref, silu_ref, slope_ref, gate_ref, up_ref, down_ref, out_ref, rows, d_gate, d_up):
+def backward_kernel(
+    msg_ref, silu_ref, slope_ref, gate_ref, up_ref, down_ref, inner_ref, ids_ref, scores_ref,
+    out_ref, grad_scores_ref, rows, d_gate, d_up,
+):
+    write_score_grad(inner_ref[...], ids_ref[...], scores_ref[...], grad_scores_ref)
     unpack(msg_ref, rows)
     for n in range(0, H, 256):
         lanes = slice(n, n + 256)
@@ -193,8 +208,7 @@
 
 
 def combine_kernel(
-    msg_ref, mix_ref, spread_ref, teacher_ref, ids_ref, scores_ref, student_hbm, grad_scores_ref, out_ref,
-    last, sent_last, student, inner, sems,
+    msg_ref, mix_ref, spread_ref, teacher_ref, student_hbm, inner, out_ref, last, sent_last, student, sems,
 ):
     copies = Copies(sems)
     unpack_last(msg_ref, last)
@@ -215,27 +229,18 @@
             inner[part, :] = partial if tile is TILES[0] else inner[part, :] + partial
         put(out_ref, sent_last, lanes, grad_out.astype(BF))
     pack_last(out_ref, sent_last)
-    hits, here = slots_of(ids_ref[...])
-    slot_inner = jnp.where(here, jnp.sum(inner[...], axis=1, keepdims=True), 0.0)
-    sigma, total = gates_of(scores_ref[...])
-    weight = (2.5 * sigma / total).astype(BF).astype(F32)
-    weighted_inner = jnp.concatenate(
-        [jnp.sum(hits[k] * slot_inner, axis=0, keepdims=True) for k in range(K)], axis=0
-    )
-    grad_w = weighted_inner / weight
-    inner_sum = jnp.sum(grad_w * sigma, axis=0, keepdims=True)
-    grad_scores_ref[...] = 2.5 * sigma * (1.0 - sigma) * (grad_w / total - inner_sum / (total * total))
     wait_all(sent)
 
 
-def gather_kernel(msg_ref, sum_ref, out_hbm, last, out, sems):
+def gather_kernel(msg_ref, mix_ref, out_hbm, last, held, out, sems):
     copies = Copies(sems)
+    held[...] = one_hot(mix_ref[...].astype(F32) > 0.0)
     unpack_last(msg_ref, last)
     lines = lines_of(msg_ref)
     sent = []
     for tile in TILES:
         lanes = lanes_of(tile)
-        out[:, lanes] = summed_rows(sum_ref, lines, last, lanes).astype(BF)
+        out[:, lanes] = summed_rows(held, lines, last, lanes).astype(BF)
         sent.append(copies.start(out.at[:, lanes], out_hbm.at[:, lanes]))
     wait_all(sent)
 
@@ -281,39 +286,43 @@
 
 def dispatch(ids, scores, scales, codes):
     return own(
-        dispatch_kernel, "dispatch", (MSG, struct((ROWS, T)), struct((T, ROWS)), struct((T, ROWS))),
+        dispatch_kernel, "dispatch", (MSG, struct((ROWS, T)), struct((T, ROWS))),
         [vmem((K, T), jnp.int32), vmem((K, T), F32), vmem((LANE, T), F32), vmem((T, D)), LAST_SCRATCH, copy_sems(6)],
-        9, (60 * 10**9, 6 * 10**6), [IN_HBM] * 4, (ON_CHIP,) * 4,
+        10, (60 * 10**9, 6 * 10**6), [IN_HBM] * 4, (ON_CHIP,) * 3,
     )(in_hbm(ids), in_hbm(scores), in_hbm(scales), in_hbm(codes))
 
 
 def forward(msg, gate, up, down):
     return own(
         forward_kernel, "expert_forward", (MSG, HID, HID), [ROWS_SCRATCH, vmem((ROWS, H))],
-        9, (15 * 10**9, 10**7), [ON_CHIP] * 4, (ON_CHIP,) * 3,
+        11, (15 * 10**9, 10**7), [ON_CHIP] * 4, (ON_CHIP,) * 3,
     )(on_chip(msg), on_chip(gate), on_chip(up), on_chip(down))
 
 
-def backward(msg, silu, slope, gate, up, down):
-    return own(
-        backward_kernel, "expert_backward", MSG, [ROWS_SCRATCH, vmem((ROWS, H)), vmem((ROWS, H))],
-        11, (15 * 10**9, 3 * 10**7), [ON_CHIP] * 6, ON_CHIP,
-    )(on_chip(msg), on_chip(silu), on_chip(slope), on_chip(gate), on_chip(up), on_chip(down))
-
-
-def combine(msg, mix, spread, teacher, ids, scores):
-    return own(
-        combine_kernel, "combine", (TOK_HBM, struct((K, T), F32), MSG),
-        [LAST_SCRATCH, LAST_SCRATCH, vmem((T, D)), vmem((ROWS, LANE), F32), copy_sems(3)],
-        9, (60 * 10**9, 10**7), [ON_CHIP] * 6, (IN_HBM, ON_CHIP, ON_CHIP),
-    )(on_chip(msg), on_chip(mix), on_chip(spread), on_chip(teacher), on_chip(ids), on_chip(scores))
-
-
-def gather(msg, sums):
-    return own(
-        gather_kernel, "gather_tokens", TOK_HBM, [LAST_SCRATCH, vmem((T, D)), copy_sems(3)],
-        8, (2 * 10**9, 6 * 10**6), [ON_CHIP] * 2, IN_HBM,
-    )(on_chip(msg), on_chip(sums))
+def backward(msg, silu, slope, gate, up, down, inner, ids, scores):
+    return own(
+        backward_kernel, "expert_backward", (MSG, struct((K, T), F32)),
+        [ROWS_SCRATCH, vmem((ROWS, H)), vmem((ROWS, H))],
+        13, (15 * 10**9, 3 * 10**7), [ON_CHIP] * 9, (ON_CHIP,) * 2,
+    )(
+        on_chip(msg), on_chip(silu), on_chip(slope), on_chip(gate), on_chip(up), on_chip(down),
+        on_chip(inner), on_chip(ids), on_chip(scores),
+    )
+
+
+def combine(msg, mix, spread, teacher):
+    return own(
+        combine_kernel, "combine", (TOK_HBM, struct((ROWS, LANE), F32), MSG),
+        [LAST_SCRATCH, LAST_SCRATCH, vmem((T, D)), copy_sems(3)],
+        10, (60 * 10**9, 10**7), [ON_CHIP] * 4, (IN_HBM, ON_CHIP, ON_CHIP),
+    )(on_chip(msg), on_chip(mix), on_chip(spread), on_chip(teacher))
+
+
+def gather(msg, mix):
+    return own(
+        gather_kernel, "gather_tokens", TOK_HBM, [LAST_SCRATCH, vmem((T, ROWS)), vmem((T, D)), copy_sems(3)],
+        9, (2 * 10**9, 6 * 10**6), [ON_CHIP] * 2, IN_HBM,
+    )(on_chip(msg), on_chip(mix))
 
 
 def exchange(msg):
@@ -324,11 +333,11 @@
     ids = expert_ids.T
     scores = route_scores.T
     gate, up, down = w_gate[0], w_up[0], w_down[0]
-    msg, spread, mix, sums = dispatch(ids, scores, block_scales.T, token_codes)
+    msg, spread, mix = dispatch(ids, scores, block_scales.T, token_codes)
     out_msg, silu, slope = forward(exchange(msg), gate, up, down)
-    student_out, grad_scores, grad_msg = combine(exchange(out_msg), mix, spread, teacher, ids, scores)
-    grad_back = backward(exchange(grad_msg), silu, slope, gate, up, down)
-    grad_tokens = gather(exchange(grad_back), sums)
+    student_out, inner, grad_msg = combine(exchange(out_msg), mix, spread, teacher)
+    grad_back, grad_scores = backward(exchange(grad_msg), silu, slope, gate, up, down, inner, ids, scores)
+    grad_tokens = gather(exchange(grad_back), mix)
     return student_out, grad_tokens, grad_scores.T
 
 

time: 297 us -> 297 us (level)
  no operation moved by 1% of the time
where the time goes in v7:
time: 297 us; the launch traced here: 296 us
  blocking collectives  255 us (86%)
  Pallas kernels  40.7 us (14%)
    all_to_all x4, blocking collectives, exchange(): lax.all_to_all(msg, ('group', 'local'), split_axis=0, concat_axis=0, tile...  255 us
    pallas_call x1, Pallas kernels, backward(): own(backward_kernel, 'expert_backward', (MSG, struct((K, T), F32)), [ROWS...  15.7 us
    pallas_call x1, Pallas kernels, forward(): own(forward_kernel, 'expert_forward', (MSG, HID, HID), [ROWS_SCRATCH, vme...  15.3 us

profile of v7, /device:TPU:1, one launch (start us, length us, event | category | flops | bytes accessed | tf_op | source)
XLA Modules:
  0.0 296.5 jit_solution(2568504775617839958)
XLA Ops:
  0.6 0.0 copy-start.1
  0.6 0.0 copy-start.2
  0.7 4.1 %dispatch.1 = (bf16[128,4,4480]{2,1,0:T(4,128)(2,1)S(1)}, bf16[640,128]{1,0:T(8,128)(2,1)S(1)}, bf16[128,640]{1,0:T(8,128)(2,1)S(1)}) custom-call(s32[4,128]{1,0:T(4,128)} %bitcast.15, f32[4,128]{1,0:T(4,128)} %bitcast.17, f32[28,128]{1,0:T(8,128)} %bitcast.19, bf16[128,3584]{1,0:T(8,128)(2,1)} %codes_hbm.1), custom_call_target="tpu_custom_call" | custom-call | flops 60000002048 | bytes 6000000 | tf_op jit(solution)/shard_map/dispatch/pallas_call | solution.py:288
  4.8 0.0 copy-start
  4.8 68.4 %all_to_all.20.msg_ref = bf16[128,4,4480]{2,1,0:T(4,128)(2,1)S(1)} all-to-all(bf16[128,4,4480]{2,1,0:T(4,128)(2,1)S(1)} %get-tuple-element.14), channel_id=1, replica_groups=mesh['group'=4,'local'=32] {'group','local'}, dimensions={0} | all-to-all | bytes 9175040 | tf_op jit(solution)/shard_map/all_to_all | solution.py:329
  73.2 0.0 copy-done.1
  73.2 0.0 copy-done.2
  73.2 0.0 copy-done
  73.2 15.3 %expert_forward.1 = (bf16[128,4,4480]{2,1,0:T(4,128)(2,1)S(1)}, bf16[640,1024]{1,0:T(8,128)(2,1)S(1)}, bf16[640,1024]{1,0:T(8,128)(2,1)S(1)}) custom-call(bf16[128,4,4480]{2,1,0:T(4,128)(2,1)S(1)} %all_to_all.20.msg_ref, bf16[3584,1024]{1,0:T(8,128)(2,1)S(1)} %bitcast.7, bf16[3584,1024]{1,0:T(8,128)(2,1)S(1)} %bitcast.9, bf16[1024,3584]{1,0:T(8,128)(2,1)S(1)} %bitcast.11), custom_call_target="tpu_custom_call" | custom-call | flops 15000000512 | bytes 10000000 | tf_op jit(solution)/shard_map/expert_forward/pallas_call | solution.py:296
  88.4 0.0 copy-start.3
  88.5 0.0 slice-start
  88.5 62.2 %all_to_all.21.msg_ref = bf16[128,4,4480]{2,1,0:T(4,128)(2,1)S(1)} all-to-all(bf16[128,4,4480]{2,1,0:T(4,128)(2,1)S(1)} %get-tuple-element.15), channel_id=1, replica_groups=mesh['group'=4,'local'=32] {'group','local'}, dimensions={0} | all-to-all | bytes 9175040 | tf_op jit(solution)/shard_map/all_to_all | solution.py:329
  150.6 0.0 copy-done.3
  150.6 0.0 slice-start.1
  150.6 3.5 %combine.1 = (bf16[128,3584]{1,0:T(8,128)(2,1)}, f32[640,128]{1,0:T(8,128)S(1)}, bf16[128,4,4480]{2,1,0:T(4,128)(2,1)S(1)}) custom-call(bf16[128,4,4480]{2,1,0:T(4,128)(2,1)S(1)} %all_to_all.21.msg_ref, bf16[128,640]{1,0:T(8,128)(2,1)S(1)} %get-tuple-element.16.mix_ref, bf16[640,128]{1,0:T(8,128)(2,1)S(1)} %get-tuple-element.17.spread_ref, ...), custom_call_target="tpu_custom_call" | custom-call | flops 60000002048 | bytes 10000000 | tf_op jit(solution)/shard_map/combine/pallas_call | solution.py:314
  154.2 0.0 copy-start.4
  154.2 0.0 copy-start.5
  154.2 62.1 %all_to_all.22.msg_ref = bf16[128,4,4480]{2,1,0:T(4,128)(2,1)S(1)} all-to-all(bf16[128,4,4480]{2,1,0:T(4,128)(2,1)S(1)} %get-tuple-element.19), channel_id=1, replica_groups=mesh['group'=4,'local'=32] {'group','local'}, dimensions={0} | all-to-all | bytes 9175040 | tf_op jit(solution)/shard_map/all_to_all | solution.py:329
  216.3 0.0 slice-done
  216.3 0.0 slice-done.1
  216.3 0.0 copy-done.4
  216.3 0.0 copy-done.5
  216.3 15.7 %expert_backward.1 = (bf16[128,4,4480]{2,1,0:T(4,128)(2,1)S(1)}, f32[4,128]{1,0:T(4,128)}) custom-call(bf16[128,4,4480]{2,1,0:T(4,128)(2,1)S(1)} %all_to_all.22.msg_ref, bf16[640,1024]{1,0:T(8,128)(2,1)S(1)} %get-tuple-element.20.silu_ref, bf16[640,1024]{1,0:T(8,128)(2,1)S(1)} %get-tuple-element.21.slope_ref, bf16[3584,1024]{1,0:T(8,128)(2,1)S(1)} %bitcast.8, ...), custom_call_target="tpu_custom_call" | custom-call | flops 15000000512 | bytes 30000000 | tf_op jit(solution)/shard_map/expert_backward/pallas_call | solution.py:303
  232.1 62.2 %all_to_all.23.msg_ref = bf16[128,4,4480]{2,1,0:T(4,128)(2,1)S(1)} all-to-all(bf16[128,4,4480]{2,1,0:T(4,128)(2,1)S(1)} %get-tuple-element.23), channel_id=1, replica_groups=mesh['group'=4,'local'=32] {'group','local'}, dimensions={0} | all-to-all | bytes 9175040 | tf_op jit(solution)/shard_map/all_to_all | solution.py:329
  294.2 2.1 gather_tokens.1
  (1 shorter events, 0.0 us)
Async XLA Ops:
  0.6 72.5 %copy-start.1 = (bf16[1,3584,1024]{2,1,0:T(8,128)(2,1)S(1)}, bf16[1,3584,1024]{2,1,0:T(8,128)(2,1)}, u32[]{:S(2)}) copy-start(bf16[1,3584,1024]{2,1,0:T(8,128)(2,1)} %param.13) | copy-start | bytes 22020100
  0.6 72.5 %copy-start.2 = (bf16[1,1024,3584]{2,1,0:T(8,128)(2,1)S(1)}, bf16[1,1024,3584]{2,1,0:T(8,128)(2,1)}, u32[]{:S(2)}) copy-start(bf16[1,1024,3584]{2,1,0:T(8,128)(2,1)} %param.14) | copy-start | bytes 22020100
  4.8 68.4 %copy-start = (bf16[1,3584,1024]{2,1,0:T(8,128)(2,1)S(1)}, bf16[1,3584,1024]{2,1,0:T(8,128)(2,1)}, u32[]{:S(2)}) copy-start(bf16[1,3584,1024]{2,1,0:T(8,128)(2,1)} %param.12) | copy-start | bytes 22020100
  88.4 62.2 %copy-start.3 = (bf16[128,3584]{1,0:T(8,128)(2,1)S(1)}, bf16[128,3584]{1,0:T(8,128)(2,1)}, u32[]{:S(2)}) copy-start(bf16[128,3584]{1,0:T(8,128)(2,1)} %teacher_ref.1) | copy-start | bytes 2752516
  88.5 127.9 %slice-start = ((s8[7340032]{0:T(1024)(128)(4,1)}), s8[4194304]{0:T(1024)(128)(4,1)S(1)}, s32[]{:S(2)}) async-start(s8[7340032]{0:T(1024)(128)(4,1)} %bitcast.12), calls=%async_computation.4 | async-start | bytes 8388608
  150.6 65.7 %slice-start.1 = ((s8[7340032]{0:T(1024)(128)(4,1)}), s8[3145728]{0:T(1024)(128)(4,1)S(1)}, s32[]{:S(2)}) async-start(s8[7340032]{0:T(1024)(128)(4,1)} %bitcast.12), calls=%async_computation.5 | async-start | bytes 6291456
  154.2 62.2 %copy-start.4 = (s32[128,4]{0,1:T(4,128)S(1)}, s32[128,4]{0,1:T(4,128)}, u32[]{:S(2)}) copy-start(s32[128,4]{0,1:T(4,128)} %param.11) | copy-start | bytes 6148
  154.2 62.2 %copy-start.5 = (f32[128,4]{0,1:T(4,128)S(1)}, f32[128,4]{0,1:T(4,128)}, u32[]{:S(2)}) copy-start(f32[128,4]{0,1:T(4,128)} %param.10) | copy-start | bytes 6148

commit v8 on v7

--- a/solution.py
+++ b/solution.py
@@ -129,16 +129,6 @@
     ids_copy.wait()
     hits, here = slots_of(ids[...])
     pick = one_hot(here)
-    scales_copy.wait()
-    scale = scales[...].T
-    for tile, copy in zip(TILES, code_copies):
-        copy.wait()
-        for j in range(tile[0], tile[0] + tile[1]):
-            lanes = lanes_of((j, 1))
-            codes[:, lanes] = (codes[:, lanes].astype(F32) * scale[:, j:j + 1]).astype(BF)
-        lanes = lanes_of(tile)
-        put(msg_ref, last, lanes, jnp.dot(pick, codes[:, lanes], preferred_element_type=F32).astype(BF))
-    pack_last(msg_ref, last)
     scores_copy.wait()
     sigma, total = gates_of(scores[...])
     weight = (2.5 * sigma / total).astype(BF).astype(F32)
@@ -149,6 +139,16 @@
     spread_ref[...] = spread.astype(BF)
     for n in range(0, ROWS, T):
         mix_ref[:, n:n + T] = spread[n:n + T].T.astype(BF)
+    scales_copy.wait()
+    scale = scales[...].T
+    for tile, copy in zip(TILES, code_copies):
+        copy.wait()
+        for j in range(tile[0], tile[0] + tile[1]):
+            lanes = lanes_of((j, 1))
+            codes[:, lanes] = (codes[:, lanes].astype(F32) * scale[:, j:j + 1]).astype(BF)
+        lanes = lanes_of(tile)
+        put(msg_ref, last, lanes, jnp.dot(pick, codes[:, lanes], preferred_element_type=F32).astype(BF))
+    pack_last(msg_ref, last)
 
 
 def write_score_grad(inner, ids, scores, grad_scores_ref):

time: 297 us -> 297 us (level)
  no operation moved by 1% of the time
where the time goes in v8:
time: 297 us; the launch traced here: 296 us
  blocking collectives  255 us (86%)
  Pallas kernels  40.7 us (14%)
    all_to_all x4, blocking collectives, exchange(): lax.all_to_all(msg, ('group', 'local'), split_axis=0, concat_axis=0, tile...  255 us
    pallas_call x1, Pallas kernels, backward(): own(backward_kernel, 'expert_backward', (MSG, struct((K, T), F32)), [ROWS...  15.7 us
    pallas_call x1, Pallas kernels, forward(): own(forward_kernel, 'expert_forward', (MSG, HID, HID), [ROWS_SCRATCH, vme...  15.3 us

profile of v8, /device:TPU:1, one launch (start us, length us, event | category | flops | bytes accessed | tf_op | source)
XLA Modules:
  0.0 296.5 jit_solution(15636820751477090697)
XLA Ops:
  0.6 0.0 copy-start.1
  0.6 0.0 copy-start.2
  0.7 4.1 %dispatch.1 = (bf16[128,4,4480]{2,1,0:T(4,128)(2,1)S(1)}, bf16[640,128]{1,0:T(8,128)(2,1)S(1)}, bf16[128,640]{1,0:T(8,128)(2,1)S(1)}) custom-call(s32[4,128]{1,0:T(4,128)} %bitcast.15, f32[4,128]{1,0:T(4,128)} %bitcast.17, f32[28,128]{1,0:T(8,128)} %bitcast.19, bf16[128,3584]{1,0:T(8,128)(2,1)} %codes_hbm.1), custom_call_target="tpu_custom_call" | custom-call | flops 60000002048 | bytes 6000000 | tf_op jit(solution)/shard_map/dispatch/pallas_call | solution.py:288
  4.8 0.0 copy-start
  4.8 68.4 %all_to_all.20.msg_ref = bf16[128,4,4480]{2,1,0:T(4,128)(2,1)S(1)} all-to-all(bf16[128,4,4480]{2,1,0:T(4,128)(2,1)S(1)} %get-tuple-element.14), channel_id=1, replica_groups=mesh['group'=4,'local'=32] {'group','local'}, dimensions={0} | all-to-all | bytes 9175040 | tf_op jit(solution)/shard_map/all_to_all | solution.py:329
  73.2 0.0 copy-done.1
  73.2 0.0 copy-done.2
  73.2 0.0 copy-done
  73.2 15.3 %expert_forward.1 = (bf16[128,4,4480]{2,1,0:T(4,128)(2,1)S(1)}, bf16[640,1024]{1,0:T(8,128)(2,1)S(1)}, bf16[640,1024]{1,0:T(8,128)(2,1)S(1)}) custom-call(bf16[128,4,4480]{2,1,0:T(4,128)(2,1)S(1)} %all_to_all.20.msg_ref, bf16[3584,1024]{1,0:T(8,128)(2,1)S(1)} %bitcast.7, bf16[3584,1024]{1,0:T(8,128)(2,1)S(1)} %bitcast.9, bf16[1024,3584]{1,0:T(8,128)(2,1)S(1)} %bitcast.11), custom_call_target="tpu_custom_call" | custom-call | flops 15000000512 | bytes 10000000 | tf_op jit(solution)/shard_map/expert_forward/pallas_call | solution.py:296
  88.5 0.0 copy-start.3
  88.5 0.0 slice-start
  88.5 62.1 %all_to_all.21.msg_ref = bf16[128,4,4480]{2,1,0:T(4,128)(2,1)S(1)} all-to-all(bf16[128,4,4480]{2,1,0:T(4,128)(2,1)S(1)} %get-tuple-element.15), channel_id=1, replica_groups=mesh['group'=4,'local'=32] {'group','local'}, dimensions={0} | all-to-all | bytes 9175040 | tf_op jit(solution)/shard_map/all_to_all | solution.py:329
  150.6 0.0 copy-done.3
  150.6 0.0 slice-start.1
  150.6 3.5 %combine.1 = (bf16[128,3584]{1,0:T(8,128)(2,1)}, f32[640,128]{1,0:T(8,128)S(1)}, bf16[128,4,4480]{2,1,0:T(4,128)(2,1)S(1)}) custom-call(bf16[128,4,4480]{2,1,0:T(4,128)(2,1)S(1)} %all_to_all.21.msg_ref, bf16[128,640]{1,0:T(8,128)(2,1)S(1)} %get-tuple-element.16.mix_ref, bf16[640,128]{1,0:T(8,128)(2,1)S(1)} %get-tuple-element.17.spread_ref, ...), custom_call_target="tpu_custom_call" | custom-call | flops 60000002048 | bytes 10000000 | tf_op jit(solution)/shard_map/combine/pallas_call | solution.py:314
  154.2 0.0 copy-start.4
  154.2 0.0 copy-start.5
  154.2 62.1 %all_to_all.22.msg_ref = bf16[128,4,4480]{2,1,0:T(4,128)(2,1)S(1)} all-to-all(bf16[128,4,4480]{2,1,0:T(4,128)(2,1)S(1)} %get-tuple-element.19), channel_id=1, replica_groups=mesh['group'=4,'local'=32] {'group','local'}, dimensions={0} | all-to-all | bytes 9175040 | tf_op jit(solution)/shard_map/all_to_all | solution.py:329
  216.3 0.0 slice-done
  216.3 0.0 slice-done.1
  216.3 0.0 copy-done.4
  216.3 0.0 copy-done.5
  216.3 15.7 %expert_backward.1 = (bf16[128,4,4480]{2,1,0:T(4,128)(2,1)S(1)}, f32[4,128]{1,0:T(4,128)}) custom-call(bf16[128,4,4480]{2,1,0:T(4,128)(2,1)S(1)} %all_to_all.22.msg_ref, bf16[640,1024]{1,0:T(8,128)(2,1)S(1)} %get-tuple-element.20.silu_ref, bf16[640,1024]{1,0:T(8,128)(2,1)S(1)} %get-tuple-element.21.slope_ref, bf16[3584,1024]{1,0:T(8,128)(2,1)S(1)} %bitcast.8, ...), custom_call_target="tpu_custom_call" | custom-call | flops 15000000512 | bytes 30000000 | tf_op jit(solution)/shard_map/expert_backward/pallas_call | solution.py:303
  232.1 62.2 %all_to_all.23.msg_ref = bf16[128,4,4480]{2,1,0:T(4,128)(2,1)S(1)} all-to-all(bf16[128,4,4480]{2,1,0:T(4,128)(2,1)S(1)} %get-tuple-element.23), channel_id=1, replica_groups=mesh['group'=4,'local'=32] {'group','local'}, dimensions={0} | all-to-all | bytes 9175040 | tf_op jit(solution)/shard_map/all_to_all | solution.py:329
  294.2 2.1 gather_tokens.1
  (1 shorter events, 0.0 us)
Async XLA Ops:
  0.6 72.5 %copy-start.1 = (bf16[1,3584,1024]{2,1,0:T(8,128)(2,1)S(1)}, bf16[1,3584,1024]{2,1,0:T(8,128)(2,1)}, u32[]{:S(2)}) copy-start(bf16[1,3584,1024]{2,1,0:T(8,128)(2,1)} %param.13) | copy-start | bytes 22020100
  0.6 72.5 %copy-start.2 = (bf16[1,1024,3584]{2,1,0:T(8,128)(2,1)S(1)}, bf16[1,1024,3584]{2,1,0:T(8,128)(2,1)}, u32[]{:S(2)}) copy-start(bf16[1,1024,3584]{2,1,0:T(8,128)(2,1)} %param.14) | copy-start | bytes 22020100
  4.8 68.4 %copy-start = (bf16[1,3584,1024]{2,1,0:T(8,128)(2,1)S(1)}, bf16[1,3584,1024]{2,1,0:T(8,128)(2,1)}, u32[]{:S(2)}) copy-start(bf16[1,3584,1024]{2,1,0:T(8,128)(2,1)} %param.12) | copy-start | bytes 22020100
  88.5 62.2 %copy-start.3 = (bf16[128,3584]{1,0:T(8,128)(2,1)S(1)}, bf16[128,3584]{1,0:T(8,128)(2,1)}, u32[]{:S(2)}) copy-start(bf16[128,3584]{1,0:T(8,128)(2,1)} %teacher_ref.1) | copy-start | bytes 2752516
  88.5 127.8 %slice-start = ((s8[7340032]{0:T(1024)(128)(4,1)}), s8[4194304]{0:T(1024)(128)(4,1)S(1)}, s32[]{:S(2)}) async-start(s8[7340032]{0:T(1024)(128)(4,1)} %bitcast.12), calls=%async_computation.4 | async-start | bytes 8388608
  150.6 65.7 %slice-start.1 = ((s8[7340032]{0:T(1024)(128)(4,1)}), s8[3145728]{0:T(1024)(128)(4,1)S(1)}, s32[]{:S(2)}) async-start(s8[7340032]{0:T(1024)(128)(4,1)} %bitcast.12), calls=%async_computation.5 | async-start | bytes 6291456
  154.2 62.2 %copy-start.4 = (s32[128,4]{0,1:T(4,128)S(1)}, s32[128,4]{0,1:T(4,128)}, u32[]{:S(2)}) copy-start(s32[128,4]{0,1:T(4,128)} %param.11) | copy-start | bytes 6148
  154.2 62.2 %copy-start.5 = (f32[128,4]{0,1:T(4,128)S(1)}, f32[128,4]{0,1:T(4,128)}, u32[]{:S(2)}) copy-start(f32[128,4]{0,1:T(4,128)} %param.10) | copy-start | bytes 6148
